TPU v7x, 512 devices: a whole 4x8x8 slice. The times are simulated.
512 devices in a mesh: sect: 4 (over z_lo, core), blk: 128 (over z_hi, x, y).
Axes of the slice: x: 4, y: 8, z: 8 (z_hi: 4, z_lo: 2; z = z_hi * 2 + z_lo), core: 2. Of those that a mesh axis runs over, the one named last changes fastest.
Arguments:
- last_perceptron_activations: bfloat16 [512, 192, 4304], P(('sect', 'blk')), may hold values from -6 to 6
- caption_reduction_matrix: bfloat16 [4304, 1152], P(None, 'blk'), may hold values from -0.09375 to 0.09375
- picture_reduction_matrix: bfloat16 [4304, 1152], P(None, 'blk'), may hold values from -0.09375 to 0.09375
- caption_offset_vector: float32 [1152], replicated, may hold values from -0.6 to 0.6
- picture_offset_vector: float32 [1152], replicated, may hold values from -0.6 to 0.6
- score_multiplier_array: float32 [1], replicated, may hold values from 4 to 16
- match_score_offset: float32 [1], replicated, may hold values from -6 to -2
- caption_match_position: int32 [384], replicated, may hold values from 0 to 383, each once
Outputs:
- text_grad: float32 [384, 4304], P('blk', 'sect')
Inputs may be any that keep to these rules, and one draw needn't show every extreme that they name: `caption_match_position`: each text index appears exactly once, so every image has exactly one paired text.
All inputs are finite; a program needn't handle non-finite values.
Results may differ from a plain program's by a relative error of at most 0.013.
Values may be sent and summed in bfloat16 or wider, within the bound.
A program may use at most 128 MiB of HBM per device.

v0:
```python
import jax
import jax.numpy as jnp
from jax import lax
from jax.sharding import Mesh
from jax.sharding import PartitionSpec as P

D = 1152
FF = 4304
TXT_LEN = 64
IMG_TOK = 192
BLK = ("blk_0", "blk_1", "blk_2")
SECT_BLK = ("sect", "blk_0", "blk_1", "blk_2")


def broadcast(x, axis, root):
    return lax.dynamic_index_in_dim(lax.all_gather(x, axis), root, 0, keepdims=False)


def joined_along(parts, dim):
    lengths = list(parts.shape[1:])
    lengths[dim] *= parts.shape[0]
    return jnp.moveaxis(parts, 0, dim).reshape(lengths)


def gather_in_order(x, axes, sequence):
    parts = x[None]
    for k in sequence:
        parts = lax.all_gather(parts, axes[k], axis=0, tiled=True)
    held = [lax.axis_size(axes[k]) for k in reversed(sequence)]
    parts = parts.reshape(*held, *x.shape)
    turned = sorted(range(len(sequence)), key=lambda place: sequence[len(sequence) - 1 - place])
    return parts.transpose(*turned, *range(len(sequence), parts.ndim)).reshape(-1, *x.shape)


def gathered_by_axis(x, axes, sequence, dim):
    return joined_along(gather_in_order(x, axes, sequence), dim)


def reduced_to_own(parts, axes, sequence):
    inside = parts.shape[1:]
    parts = parts.reshape(*(lax.axis_size(a) for a in axes), *inside)
    parts = jnp.moveaxis(parts, sequence, range(len(axes))).reshape(-1, *inside)
    for k in sequence:
        parts = lax.psum_scatter(parts, axes[k], scatter_dimension=0, tiled=True)
    return parts[0]


def cut_along(x, dim, count):
    before, after = (x.shape[:dim], x.shape[dim + 1 :])
    return jnp.moveaxis(x.reshape(*before, count, -1, *after), dim, 0)


def summed_rows(x, axes, sequence, dim):
    count = lax.axis_size(axes)
    return reduced_to_own(cut_along(x, dim, count), axes, sequence)


def copy_for_each(x, axis):
    count = lax.axis_size(axis)
    return lax.all_to_all(jnp.broadcast_to(x[None], (count, *x.shape)), axis, 0, 0, tiled=True)


def of_everyone(x, axis):
    return copy_for_each(x, axis).sum(axis=0)


def unit_rows(pool):
    inv = lax.rsqrt(jnp.sum(pool * pool, axis=-1, keepdims=True) + 1e-06)
    return (pool * inv, inv)


def on_device(
    last_perceptron_activations,
    caption_reduction_matrix,
    picture_reduction_matrix,
    caption_offset_vector,
    picture_offset_vector,
    score_multiplier_array,
    match_score_offset,
    caption_match_position,
):
    hidden = last_perceptron_activations[0]
    sect_index = lax.axis_index("sect")
    blk_index = lax.axis_index(BLK)
    blk_count = lax.axis_size(BLK)
    sect_count = lax.axis_size("sect")
    rows = hidden.shape[0]
    txt_count = rows // TXT_LEN
    img_count = rows // IMG_TOK
    width = FF // sect_count
    is_text = sect_index == 0
    live = jnp.where(is_text, 0.0, 1.0).astype(jnp.float32)
    w_local = jnp.where(is_text, caption_reduction_matrix, picture_reduction_matrix)
    outs = jnp.dot(
        hidden, lax.all_gather(w_local, BLK, axis=1, tiled=True), preferred_element_type=jnp.float32
    )
    text_pool = jnp.mean(outs.reshape(txt_count, TXT_LEN, D), axis=1) + caption_offset_vector
    image_pool = jnp.mean(outs.reshape(img_count, IMG_TOK, D), axis=1) + picture_offset_vector
    text_pool = broadcast(text_pool, "sect", 0)
    text_unit, text_inv = unit_rows(text_pool)
    image_unit, image_inv = unit_rows(image_pool)
    text_emb = text_unit.astype(jnp.bfloat16)
    image_emb = image_unit.astype(jnp.bfloat16)
    similarity_multiplier = score_multiplier_array[0]
    shift_bias = match_score_offset[0]
    first = jnp.maximum((sect_index - 1) * blk_count + blk_index, 0) * img_count
    mine = lax.dynamic_slice_in_dim(caption_match_position, first, img_count)
    all_texts = gathered_by_axis(text_emb, BLK, (0, 1, 2), 0)
    count = all_texts.shape[0]
    logits = (
        similarity_multiplier
        * lax.dot_general(
            image_emb, all_texts, (((1,), (1,)), ((), ())), preferred_element_type=jnp.float32
        )
        + shift_bias
    )
    index_row = jnp.arange(count, dtype=jnp.int32)
    label = jnp.where(mine[:, None] == index_row[None, :], 1.0, -1.0).astype(jnp.float32)
    coef = (-label * jax.nn.sigmoid(-label * logits) * live).astype(jnp.bfloat16)
    acc_full = lax.dot_general(
        coef, image_emb, (((0,), (0,)), ((), ())), preferred_element_type=jnp.float32
    )
    acc = summed_rows(acc_full, BLK, (1, 2, 0), 0)
    acc = of_everyone(acc, "sect")
    grad = similarity_multiplier * acc
    grad_pool = (grad - text_unit * jnp.sum(text_unit * grad, axis=-1, keepdims=True)) * text_inv
    dy = grad_pool.astype(jnp.bfloat16)
    w_rows = lax.dynamic_slice_in_dim(caption_reduction_matrix, sect_index * width, width, 0)
    return lax.dot_general(
        dy,
        gathered_by_axis(w_rows, BLK, (0, 1, 2), 1),
        (((1,), (1,)), ((), ())),
        preferred_element_type=jnp.float32,
    )


def solution(mesh):
    finer = Mesh(
        mesh.devices.reshape(mesh.shape["sect"], 4, 4, 8), ("sect", "blk_0", "blk_1", "blk_2")
    )
    placed = (P(SECT_BLK, None, None), P(None, BLK), P(None, BLK), P(), P(), P(), P(), P())
    return jax.shard_map(
        on_device, mesh=finer, in_specs=placed, out_specs=P(BLK, "sect"), check_vma=False
    )
```

profile of v0, /device:TPU:1, one launch (start us, length us, event | category | flops | bytes accessed | tf_op | source)
XLA Modules:
  0.0 509.8 jit_solution(2313802400999751418)
XLA Ops:
  6.5 1.7 select_bitcast_fusion
  9.6 1.3 dynamic_slice.10
  10.9 225.4 %all-gather.8.cloned.1.call-done = bf16[128,9,4304]{2,1,0:T(8,128)(2,1)} async-done(((bf16[1,9,4304]{2,1,0:T(8,128)(2,1)}), bf16[128,9,4304]{2,1,0:T(8,128)(2,1)}) %all-gather.8.cloned.1.call-update) | async-done | bytes 9916432 | tf_op jit(solution)/shard_map/all_gather | solution.py:95
  236.4 17.9 %reshape.152 = bf16[1152,4304]{1,0:T(8,128)(2,1)} reshape(bf16[128,9,4304]{2,1,0:T(8,128)(2,1)} %all-gather.8.cloned.1.call-done) | data formatting | bytes 19832832
  254.2 7.3 %fusion.14 = (f32[1152]{0:T(1024)S(1)}, f32[1152,192]{0,1:T(8,128)S(1)}) fusion(bf16[1152,4304]{1,0:T(8,128)(2,1)} %reshape.152, bf16[1,192,4304]{2,1,0:T(8,128)(2,1)S(1)} %copy-done), kind=kOutput, calls=%fused_computation.32 | convolution fusion | flops 1904171904 | bytes 12458496 | tf_op jit(solution)/shard_map/dot_general | solution.py:94
  261.6 6.5 %all_gather.26 = f32[4,3,1152]{2,1,0:T(4,128)S(1)} all-gather(f32[1,3,1152]{2,1,0:T(4,128)S(1)} %bitcast_add_fusion), channel_id=1, replica_groups=mesh['sect'=4,'blk_0'=4,'blk_1'=4,'blk_2'=8] {'sect'}, dimensions={0}, use_global_device_ids=true | all-gather | bytes 69120 | tf_op jit(solution)/shard_map/all_gather | solution.py:16
  268.3 10.9 %all_gather.27 = bf16[4,3,1152]{2,1,0:T(4,128)(2,1)S(1)} all-gather(bf16[1,3,1152]{2,1,0:T(4,128)(2,1)S(1)} %multiply_convert_fusion), channel_id=1, replica_groups=mesh['sect'=4,'blk_0'=4,'blk_1'=4,'blk_2'=8] {'blk_0'}, dimensions={0}, use_global_device_ids=true | all-gather | bytes 34560 | tf_op jit(solution)/shard_map/all_gather | solution.py:28
  279.2 9.5 %all_gather.28 = bf16[16,3,1152]{2,1,0:T(4,128)(2,1)S(1)} all-gather(bf16[4,3,1152]{2,1,0:T(4,128)(2,1)S(1)} %all_gather.27), channel_id=1, replica_groups=mesh['sect'=4,'blk_0'=4,'blk_1'=4,'blk_2'=8] {'blk_1'}, dimensions={0}, use_global_device_ids=true | all-gather | bytes 138240 | tf_op jit(solution)/shard_map/all_gather | solution.py:28
  288.7 21.0 %all_gather.29 = bf16[128,3,1152]{2,0,1:T(8,128)(2,1)S(1)} all-gather(bf16[16,3,1152]{2,0,1:T(8,128)(2,1)S(1)} %copy.34), channel_id=1, replica_groups=mesh['sect'=4,'blk_0'=4,'blk_1'=4,'blk_2'=8] {'blk_2'}, dimensions={0}, use_global_device_ids=true | all-gather | bytes 995328 | tf_op jit(solution)/shard_map/all_gather | solution.py:28
  309.7 1.1 reshape.143
  310.9 1.9 copy.35
  312.8 1.5 reshape_reshape.4
  315.7 1.5 convolution_reduce_fusion
  318.1 0.9 copy.36
  319.0 1.1 multiply_bitcast_fusion
  320.1 1.8 reshape.145
  322.0 37.7 %reduce-scatter.4.cloned.1.call-done = f32[32,3,1152]{2,0,1:T(8,128)} async-done(((f32[128,3,1152]{2,0,1:T(8,128)}), f32[32,3,1152]{2,0,1:T(8,128)}) %reduce-scatter.4.cloned.1.call-update) | async-done | bytes 442384 | tf_op jit(solution)/shard_map/reduce_scatter | solution.py:44
  359.7 0.9 dynamic-slice_bitcast_fusion
  360.6 13.9 %all-gather.2 = bf16[4,1076,9]{1,2,0:T(8,128)(2,1)S(1)} all-gather(bf16[1,1076,9]{1,2,0:T(8,128)(2,1)S(1)} %dynamic-slice_bitcast_fusion), channel_id=2, replica_groups=mesh['sect'=4,'blk_0'=4,'blk_1'=4,'blk_2'=8] {'blk_0'}, dimensions={0}, use_global_device_ids=true | all-gather | bytes 96840 | tf_op jit(solution)/shard_map/all_gather | solution.py:28
  374.5 10.4 %all_gather.31 = bf16[16,1076,9]{1,2,0:T(8,128)(2,1)S(1)} all-gather(bf16[4,1076,9]{1,2,0:T(8,128)(2,1)S(1)} %all-gather.2), channel_id=1, replica_groups=mesh['sect'=4,'blk_0'=4,'blk_1'=4,'blk_2'=8] {'blk_1'}, dimensions={0}, use_global_device_ids=true | all-gather | bytes 387360 | tf_op jit(solution)/shard_map/all_gather | solution.py:28
  384.9 0.8 copy.38
  385.8 1.3 dynamic-slice
  387.0 1.2 dynamic-slice.2
  388.9 46.6 %all-reduce.4.cloned.1.call-done = f32[32,3,1152]{2,0,1:T(8,128)} async-done(((f32[32,3,1152]{2,0,1:T(8,128)}), f32[32,3,1152]{2,0,1:T(8,128)}) %all-reduce.4.cloned.1.call-update) | async-done | bytes 442384
  435.5 0.9 constant_dynamic-slice_fusion.1
  436.4 17.5 %all-reduce.1 = f32[4,3,1152]{2,0,1:T(4,128)S(1)} all-reduce(f32[4,3,1152]{2,0,1:T(4,128)S(1)} %constant_dynamic-slice_fusion.1), channel_id=5, replica_groups=mesh['sect'=4,'blk_0'=4,'blk_1'=4,'blk_2'=8] {'blk_0'}, use_global_device_ids=true, to_apply=%region_6.7.clone | all-reduce | flops 13824 | bytes 110592
  455.2 13.2 %all-to-all-start = ((f32[4,3,1152]{2,1,0:T(4,128)}), f32[4,3,1152]{2,1,0:T(4,128)S(1)}, u32[]{:S(2)}, u32[]{:S(2)}) async-start(f32[4,3,1152]{2,1,0:T(4,128)} %broadcast_in_dim.29), calls=%async_computation.1 | async-start | bytes 147456 | tf_op jit(solution)/shard_map/all_to_all | solution.py:60
  468.4 14.7 %all-gather.6.cloned.1.call-done = bf16[128,1076,9]{1,0,2:T(8,128)(2,1)} async-done(((bf16[16,1076,9]{1,0,2:T(8,128)(2,1)}), bf16[128,1076,9]{1,0,2:T(8,128)(2,1)}) %all-gather.6.cloned.1.call-update) | async-done | bytes 2479120 | tf_op jit(solution)/shard_map/all_gather | solution.py:28
  483.1 5.6 %reshape.146 = bf16[8,4,4,1076,9]{3,2,1,0,4:T(4,128)(2,1)} reshape(bf16[128,1076,9]{1,0,2:T(8,128)(2,1)} %all-gather.6.cloned.1.call-done) | data formatting | bytes 4958208 | tf_op jit(solution)/shard_map/reshape | solution.py:30
  488.6 5.6 %copy.41 = bf16[4,4,8,1076,9]{3,4,2,1,0:T(8,128)(2,1)} copy(bf16[4,4,8,1076,9]{3,0,1,2,4:T(4,128)(2,1)} %bitcast.69) | data formatting | bytes 4958208 | tf_op jit(solution)/shard_map/transpose | solution.py:22
  494.2 5.9 %reshape.148 = bf16[1076,1152]{0,1:T(8,128)(2,1)} reshape(bf16[1076,128,9]{0,2,1:T(8,128)(2,1)} %bitcast.68) | data formatting | bytes 4958208 | tf_op jit(solution)/shard_map/reshape | solution.py:22
  500.4 2.9 fusion.7
  (31 shorter events, 3.4 us)
Async XLA Ops:
  6.5 247.7 %copy-start = (bf16[1,192,4304]{2,1,0:T(8,128)(2,1)S(1)}, bf16[1,192,4304]{2,1,0:T(8,128)(2,1)}, u32[]{:S(2)}) copy-start(bf16[1,192,4304]{2,1,0:T(8,128)(2,1)} %param.8) | copy-start | bytes 4958212
  6.5 229.8 %all-gather.8.cloned.1.call-start = ((), (), s32[]{:S(2)}) async-start(), calls=%async_computation.4 | async-start | bytes 17965056 | tf_op jit(solution)/shard_map/all_gather | solution.py:95
  8.3 351.4 %reduce-scatter.4.cloned.1.call-start = ((), (), s32[]{:S(2)}) async-start(), calls=%async_computation.2 | async-start | bytes 2211840 | tf_op jit(solution)/shard_map/reduce_scatter | solution.py:44
  254.2 7.3 %copy-start.2 = (f32[1152]{0:T(1024)S(1)}, f32[1152]{0:T(1024)}, u32[]{:S(2)}) copy-start(f32[1152]{0:T(1024)} %param.11) | copy-start | bytes 13828
  309.7 4.6 copy-start.1
  321.9 113.6 %all-reduce.4.cloned.1.call-start = ((), (), s32[]{:S(2)}) async-start(), calls=%async_computation.5 | async-start | bytes 884736
  359.7 123.4 %all-gather.6.cloned.1.call-start = ((), (), s32[]{:S(2)}) async-start(), calls=%async_computation.3 | async-start | bytes 2985984 | tf_op jit(solution)/shard_map/all_gather | solution.py:28
  455.2 45.0 %all-to-all-start = ((f32[4,3,1152]{2,1,0:T(4,128)}), f32[4,3,1152]{2,1,0:T(4,128)S(1)}, u32[]{:S(2)}, u32[]{:S(2)}) async-start(f32[4,3,1152]{2,1,0:T(4,128)} %broadcast_in_dim.29), calls=%async_computation.1 | async-start | bytes 147456 | tf_op jit(solution)/shard_map/all_to_all | solution.py:60
Sparse Core Ops, SparseCore 0:
  11.7 224.6 all-gather.7
  322.1 37.5 reduce-scatter.3
  362.0 73.4 all-reduce.3
  437.5 45.5 all-gather.5
where the time goes:
time: 513 us; the launch traced here: 510 us
  waiting for transfers between devices  324 us (63%)
  blocking collectives  89.7 us (17%)
  local copies, waits for them, and re-layouts  50.2 us (10%)
  between operations  15.9 us (3%)
  starting transfers between devices  13.3 us (3%)
  matrix products  11.7 us (2%)
    all_gather x1, waiting for transfers between devices, on_device(): lax.all_gather(w_local, BLK, axis=1, tiled=True)  225 us
    all_gather x5, blocking collectives, gather_in_order(): parts = lax.all_gather(parts, axes[k], axis=0, tiled=True)  65.7 us
    unnamed x5, waiting for transfers between devices  46.7 us
    reduce_scatter x1, waiting for transfers between devices, reduced_to_own(): parts = lax.psum_scatter(parts, axes[k], scatter_dimension=0, tiled=True)  37.7 us
    unnamed x13, local copies, waits for them, and re-layouts  22.7 us
    unnamed x1, blocking collectives  17.5 us
    all_gather x1, waiting for transfers between devices, gather_in_order(): parts = lax.all_gather(parts, axes[k], axis=0, tiled=True)  14.7 us
    all_to_all x1, starting transfers between devices, copy_for_each(): lax.all_to_all(jnp.broadcast_to(x[None], (count, *x.shape)), axis, 0, 0,...  13.2 us
  transfers between devices with their start and end apart: 5, of which 4 were waited for; matrix products, arithmetic and copies ran while one was open for 5% of the time, Pallas kernels for 0%

commit v1 on v0

v1 whole, which is shorter than its diff:
```python
import functools

import jax
import jax.numpy as jnp
from jax import lax
from jax.experimental import pallas as pl
from jax.experimental.pallas import tpu as pltpu
from jax.sharding import Mesh
from jax.sharding import PartitionSpec as P

TXT_LEN = 64
NT = 3
K8 = 8
BF = jnp.bfloat16
F32 = jnp.float32
BLK = ("blk_0", "blk_1", "blk_2")
SECT_BLK = ("sect", "blk_0", "blk_1", "blk_2")
MESH = pl.DeviceIdType.MESH


def iota(shape, dim):
    return lax.broadcasted_iota(jnp.int32, shape, dim)


def dot_nn(a, b):
    return lax.dot_general(a, b, (((1,), (0,)), ((), ())), preferred_element_type=F32)


def dot_nt(a, b):
    return lax.dot_general(a, b, (((1,), (1,)), ((), ())), preferred_element_type=F32)


def kernel(
    dims,
    hid, wt, wi, bt, bi, mult, off, pos,
    out,
    hv, wv, wtmp, wm, wx, xpad,
    hsend, hrecv, hall,
    psend, precv, full,
    pf, tbuf, emb,
    arecv, dys, dyr, osend, orecv,
    lsem, ssem, rsem, zsem,
):
    NS, NZ, NX, NY, FF = dims
    FFQ = FF // NS
    LP = wtmp.shape[1]
    NZX = NZ * NX
    NM = NZX * K8
    NE = NZX * NY
    s = lax.axis_index("sect")
    z = lax.axis_index("blk_0")
    x = lax.axis_index("blk_1")
    y = lax.axis_index("blk_2")
    zx = z * NX + x
    blk = zx * NY + y

    sect_peers = [{"sect": lax.rem(s + d, NS)} for d in range(1, NS)]
    y_peers = [{"blk_2": lax.rem(y + d, NY)} for d in range(1, NY)]
    z_peers = [{"blk_0": lax.rem(z + d, NZ)} for d in range(1, NZ)]
    x_peers = [{"blk_1": lax.rem(x + d, NX)} for d in range(1, NX)]
    zx_peers = []
    for d in range(1, NZX):
        p = lax.rem(zx + d, NZX)
        zx_peers.append({"blk_0": p // NX, "blk_1": lax.rem(p, NX)})

    loads = [
        pltpu.make_async_copy(wi, wv.at[0], lsem.at[0]),
        pltpu.make_async_copy(wt, wv.at[1], lsem.at[1]),
        pltpu.make_async_copy(hid, hv, lsem.at[2]),
    ]
    for c in loads:
        c.start()
    barrier = pltpu.get_barrier_semaphore()
    everyone = sect_peers + y_peers + zx_peers
    for p in everyone:
        pl.semaphore_signal(barrier, inc=1, device_id=p, device_id_type=MESH)

    def send(src, dst, k, peer, recv=None):
        pltpu.make_async_remote_copy(
            src_ref=src, dst_ref=dst, send_sem=ssem.at[k],
            recv_sem=rsem.at[k] if recv is None else recv,
            device_id=peer, device_id_type=MESH,
        ).start()

    def await_bytes(ref, sem):
        pltpu.make_async_copy(ref, ref, sem).wait()

    me = x * NZ + z
    for m, b in ((0, bi), (1, bt)):
        loads[m].wait()
        w32 = wv[m].astype(F32)
        wtmp[...] = jnp.zeros_like(wtmp)
        for q in range(NS):
            @pl.when(s == q)
            def _(q=q, w32=w32):
                wtmp[:, :FFQ] = w32[:, q * FFQ:(q + 1) * FFQ]
        v = wtmp[...]
        brow = jnp.broadcast_to(b[...], (K8 + 1, b.shape[1]))
        pick = iota(brow.shape, 1) == blk * (K8 + 1) + iota(brow.shape, 0)
        bcol = jnp.sum(jnp.where(pick, brow, 0.0), axis=1, keepdims=True)
        hi = bcol.astype(BF).astype(F32)
        lo = (bcol - hi).astype(BF).astype(F32)
        lane = iota(v.shape, 1)
        v = jnp.where(lane == FFQ, hi, v)
        v = jnp.where(lane == FFQ + 1, lo, v)
        v = jnp.where(lane == FFQ + 2, bcol - hi - lo, v)
        wm[me, m] = v[:K8].astype(BF)
        wx[me, m] = v[K8:].astype(BF).astype(F32)

    rows = hv.shape[0]
    r8 = iota((8, rows), 0)
    t8 = iota((8, rows), 1)
    is_txt = s == 0
    at = (lax.shift_right_logical(t8, 6) == r8).astype(F32)
    ai = (r8 == s + (NT - 1)).astype(F32)
    f_txt = is_txt.astype(F32)
    a = (f_txt * at + (1.0 - f_txt) * ai).astype(BF)
    scale = jnp.where(is_txt, 1.0 / TXT_LEN, 1.0 / rows)
    loads[2].wait()
    hsum = dot_nn(a, hv[...]) * scale
    hsend[...] = jnp.zeros_like(hsend)
    for q in range(NS):
        hsend[q, :, :FFQ] = hsum[:, q * FFQ:(q + 1) * FFQ].astype(BF)
    hrecv[s] = hsend[s]

    NI = NZX * 8
    lane_i = iota((pos.shape[1], NI), 1)
    rho = lax.bitwise_and(lane_i, 7)
    img = (
        (NZX * NY) * jnp.where(rho < NT, rho, rho - NT)
        + lax.shift_right_logical(lane_i, 3) * NY + 2 * s + jnp.where(rho < NT, 1, 0)
    )
    sel = ((iota((pos.shape[1], NI), 0) == img) & (rho < 2 * NT)).astype(F32).astype(BF)
    pv = jnp.broadcast_to(pos[...], (8, pos.shape[1]))
    p_hi = lax.shift_right_logical(pv, 4).astype(F32).astype(BF)
    p_lo = lax.bitwise_and(pv, 15).astype(F32).astype(BF)
    posl = 16.0 * dot_nn(p_hi, sel) + dot_nn(p_lo, sel)

    pl.semaphore_wait(barrier, len(everyone))

    for d in range(1, NS):
        send(hsend.at[lax.rem(s + d, NS)], hrecv.at[s], 0, sect_peers[d - 1])
    for i in range(NZ - 1):
        send(wm.at[me], wm.at[me], 1, z_peers[i], zsem.at[2 * i])
        send(wx.at[me], wx.at[me], 2, z_peers[i], zsem.at[2 * i + 1])
    for i in range(NX - 1):
        send(wm.at[me], wm.at[me], 3, x_peers[i])
        send(wx.at[me], wx.at[me], 4, x_peers[i])
    await_bytes(hrecv.at[pl.ds(0, NS - 1)], rsem.at[0])
    hq = jnp.sum(hrecv[...].astype(F32), axis=0)
    lane = iota(hq.shape, 1)
    ones = ((lane >= FFQ) & (lane < FFQ + 3)).astype(F32) * f_txt
    hall[y] = (hq + ones).astype(BF)
    for p in y_peers:
        send(hall.at[y], hall.at[y], 5, p)
    for i in range(NZ - 1):
        zz = lax.rem(z + NZ - (i + 1), NZ)
        sl = x * NZ + zz
        await_bytes(wm.at[sl], zsem.at[2 * i])
        await_bytes(wx.at[sl], zsem.at[2 * i + 1])
        for p in x_peers:
            send(wm.at[sl], wm.at[sl], 3, p)
            send(wx.at[sl], wx.at[sl], 4, p)
    await_bytes(hall.at[pl.ds(0, NY - 1)], rsem.at[5])
    hrows = hall[...].reshape(NY * 8, LP)
    nx_in = (NX - 1) * NZ
    await_bytes(wm.at[pl.ds(0, nx_in)], rsem.at[3])
    await_bytes(wx.at[pl.ds(0, nx_in)], rsem.at[4])

    xpad[...] = jnp.zeros_like(xpad)
    parts = []
    for m in range(2):
        for j in range(NZX):
            wtmp[0:1, :] = wx[j, m]
            xpad[m, 0, j:j + 1, :] = wtmp[0:1, :]
    for m in range(2):
        ext = xpad[m, 0].astype(BF)
        pm = dot_nt(hrows, wm[:, m].reshape(NM, LP))
        pe = dot_nt(hrows, ext)
        parts.append((pm, pe))
    r64 = lax.bitwise_and(iota((NY * 8, 1), 0), 7)
    pm = jnp.where(r64 < NT, parts[1][0], parts[0][0])
    pe = jnp.where(r64 < NT, parts[1][1], parts[0][1])
    place = (iota((NZX, NE), 1) == y * NZX + iota((NZX, NE), 0)).astype(F32)
    pe = lax.dot_general(
        pe, place, (((1,), (0,)), ((), ())), preferred_element_type=F32,
        precision=lax.Precision.HIGHEST,
    )
    psend[:, :, :NM] = pm.reshape(NS, 2 * 8, NM)
    psend[:, :, NM:] = pe.reshape(NS, 2 * 8, NE)
    precv[s] = psend[s]
    for d in range(1, NS):
        send(psend.at[lax.rem(s + d, NS)], precv.at[s], 6, sect_peers[d - 1])
    await_bytes(precv.at[pl.ds(0, NS - 1)], rsem.at[6])
    full[y] = jnp.sum(precv[...], axis=0)
    for p in y_peers:
        send(full.at[y], full.at[y], 7, p)
    await_bytes(full.at[pl.ds(0, NY - 1)], rsem.at[7])
    fv = full[...]
    extra = jnp.sum(fv[:, :, NM:], axis=0)
    pool = jnp.concatenate([fv[j, :, :NM] for j in range(NY)] + [extra], axis=1)
    D = pool.shape[1]
    pf[...] = pool.reshape(2, 8, D)

    def unit_rows(p):
        inv = lax.rsqrt(jnp.sum(p * p, axis=-1, keepdims=True) + 1e-06)
        return p * inv, inv

    unit, _ = unit_rows(pool)
    r8 = iota((8, 1), 0)
    both = jnp.where(r8 < NT, pltpu.roll(unit[8:], 8 - NT, 0), unit[:8])
    emb[zx] = jnp.where(r8 < 2 * NT, both, 0.0).astype(BF)
    for p in zx_peers:
        send(emb.at[zx], emb.at[zx], 8, p)
    owner = s == y // 2
    mine = pf.at[lax.rem(y, 2)]

    @pl.when(owner)
    def _():
        for i, p in enumerate(sect_peers):
            send(mine, tbuf, 13 + i, p, rsem.at[9])
        c = pltpu.make_async_copy(mine, tbuf, lsem.at[0])
        c.start()
        c.wait()

    @pl.when(jnp.logical_not(owner))
    def _():
        await_bytes(tbuf, rsem.at[9])

    t_unit, t_inv = unit_rows(tbuf[...])
    t_emb = t_unit.astype(BF)
    m_ = mult[0]
    await_bytes(emb.at[pl.ds(0, NZX - 1)], rsem.at[8])
    ev = emb[...].reshape(NI, D)
    logits = m_ * dot_nt(t_emb, ev) + off[0]
    row = iota(logits.shape, 0)
    hit = posl == (NT * blk + row).astype(F32)
    label = jnp.where(hit, 1.0, -1.0)
    coef = -label * jax.nn.sigmoid(-label * logits)
    coef = jnp.where(row < NT, coef, 0.0).astype(BF)
    acc = dot_nn(coef, ev)
    arecv[s] = acc[:4]
    for p in sect_peers:
        send(arecv.at[s], arecv.at[s], 10, p)
    await_bytes(arecv.at[pl.ds(0, NS - 1)], rsem.at[10])
    g = m_ * jnp.sum(arecv[...], axis=0)
    u = t_unit[:4]
    gp = (g - u * jnp.sum(u * g, axis=-1, keepdims=True)) * t_inv[:4]
    dy = jnp.concatenate([gp, jnp.zeros_like(gp)], axis=0).astype(BF)
    for j in range(NY):
        dys[j, :, :NM] = dy[:, j * NM:(j + 1) * NM]
        dys[j, :, NM:] = dy[:, NY * NM:]
    dyr[y] = dys[y]
    for d in range(1, NY):
        send(dys.at[lax.rem(y + d, NY)], dyr.at[y], 11, y_peers[d - 1])
    wext = xpad[1, 0].astype(BF)
    await_bytes(dyr.at[pl.ds(0, NY - 1)], rsem.at[11])
    dv = dyr[...].reshape(NY * 8, NM + NE)
    take = (iota((NE, NZX), 0) == y * NZX + iota((NE, NZX), 1)).astype(F32).astype(BF)
    dext = dot_nn(dv[:, NM:], take).astype(BF)
    o = dot_nn(dv[:, :NM], wm[:, 1].reshape(NM, LP)) + dot_nn(dext, wext)
    for j in range(NY):
        osend[j] = o[8 * j:8 * j + 4]
    orecv[y] = osend[y]
    for d in range(1, NY):
        send(osend.at[lax.rem(y + d, NY)], orecv.at[y], 12, y_peers[d - 1])
    await_bytes(orecv.at[pl.ds(0, NY - 1)], rsem.at[12])
    out[...] = jnp.sum(orecv[...], axis=0)[:NT, :FFQ]

    await_bytes(hrecv.at[pl.ds(0, NS - 1)], ssem.at[0])
    await_bytes(wm.at[pl.ds(0, NZ - 1)], ssem.at[1])
    await_bytes(wx.at[pl.ds(0, NZ - 1)], ssem.at[2])
    await_bytes(wm.at[pl.ds(0, nx_in)], ssem.at[3])
    await_bytes(wx.at[pl.ds(0, nx_in)], ssem.at[4])
    await_bytes(hall.at[pl.ds(0, NY - 1)], ssem.at[5])
    await_bytes(precv.at[pl.ds(0, NS - 1)], ssem.at[6])
    await_bytes(full.at[pl.ds(0, NY - 1)], ssem.at[7])
    await_bytes(emb.at[pl.ds(0, NZX - 1)], ssem.at[8])

    @pl.when(owner)
    def _():
        for i in range(NS - 1):
            await_bytes(tbuf, ssem.at[13 + i])

    await_bytes(arecv.at[pl.ds(0, NS - 1)], ssem.at[10])
    await_bytes(dyr.at[pl.ds(0, NY - 1)], ssem.at[11])
    await_bytes(orecv.at[pl.ds(0, NY - 1)], ssem.at[12])


def on_device(hidden, w_txt, w_img, b_txt, b_img, mult, off, pos):
    NS, NZ, NX, NY = (lax.axis_size(a) for a in SECT_BLK)
    _, rows, FF = hidden.shape
    D = b_txt.shape[0]
    K = w_txt.shape[1]
    NZX = NZ * NX
    NM, NE = NZX * K8, NZX * NY
    FFQ = FF // NS
    LP = (FFQ + 3 + 127) // 128 * 128
    dims = (NS, NZ, NX, NY, FF)
    vm = pltpu.VMEM
    scratch = [
        vm((rows, FF), BF),
        vm((2, K, FF), BF),
        vm((K, LP), F32),
        vm((NZX, 2, K8, LP), BF),
        vm((NZX, 2, 1, LP), F32),
        vm((2, 1, NZX, LP), F32),
        vm((NS, 8, LP), BF),
        vm((NS, 8, LP), BF),
        vm((NY, 8, LP), BF),
        vm((NS, 16, NM + NE), F32),
        vm((NS, 16, NM + NE), F32),
        vm((NY, 16, NM + NE), F32),
        vm((2, 8, D), F32),
        vm((8, D), F32),
        vm((NZX, 8, D), BF),
        vm((NS, 4, D), F32),
        vm((NY, 8, NM + NE), BF),
        vm((NY, 8, NM + NE), BF),
        vm((NY, 4, LP), F32),
        vm((NY, 4, LP), F32),
        pltpu.SemaphoreType.DMA((3,)),
        pltpu.SemaphoreType.DMA((12 + NS,)),
        pltpu.SemaphoreType.DMA((13,)),
        pltpu.SemaphoreType.DMA((2 * (NZ - 1),)),
    ]
    any_ = pl.BlockSpec(memory_space=pl.ANY)
    vmem = pl.BlockSpec(memory_space=pltpu.VMEM)
    smem = pl.BlockSpec(memory_space=pltpu.SMEM)
    return pl.pallas_call(
        functools.partial(kernel, dims),
        out_shape=jax.ShapeDtypeStruct((NT, FFQ), F32),
        in_specs=[any_, any_, any_, vmem, vmem, smem, smem, vmem],
        out_specs=vmem,
        scratch_shapes=scratch,
        compiler_params=pltpu.CompilerParams(collective_id=0, has_side_effects=True),
    )(
        hidden[0], w_txt.T, w_img.T, b_txt[None], b_img[None], mult, off, pos[None]
    )


def solution(mesh):
    finer = Mesh(
        mesh.devices.reshape(mesh.shape["sect"], 4, 4, 8), ("sect", "blk_0", "blk_1", "blk_2")
    )
    placed = (P(SECT_BLK, None, None), P(None, BLK), P(None, BLK), P(), P(), P(), P(), P())
    return jax.shard_map(
        on_device, mesh=finer, in_specs=placed, out_specs=P(BLK, "sect"), check_vma=False
    )
```

time: 513 us -> 70.1 us (0.14)
  waiting for transfers between devices: 324 us -> 0 us
  blocking collectives: 89.7 us -> 0 us
  Pallas kernels: 0 us -> 62.3 us
  local copies, waits for them, and re-layouts: 50.2 us -> 5.17 us
  between operations: 15.9 us -> 1.31 us
  starting transfers between devices: 13.3 us -> 0 us
  matrix products: 11.7 us -> 0 us
    all_gather x2 -> x0, waiting for transfers between devices: 240 us -> none  [the longest x1 225 us: on_device(): lax.all_gather(w_local, BLK, axis=1, tiled=True)]
    all_gather x6 -> x0, blocking collectives: 72.2 us -> none  [the longest x5 65.7 us: gather_in_order(): parts = lax.all_gather(parts, axes[k], axis=0, tiled=True)]
    pallas_call x0 -> x1, Pallas kernels: none -> 62.3 us  [on_device(): pl.pallas_call(functools.partial(kernel, dims), out_shape=jax.ShapeDtypeS...]
    unnamed x5 -> x0, waiting for transfers between devices: 46.7 us -> none
    reduce_scatter x1 -> x0, waiting for transfers between devices: 37.7 us -> none  [reduced_to_own(): parts = lax.psum_scatter(parts, axes[k], scatter_dimension=0, tiled=True)]
    unnamed x13 -> x1, local copies, waits for them, and re-layouts: 22.7 us -> 1.33 us
    unnamed x1 -> x0, blocking collectives: 17.5 us -> none
    reshape x4 -> x0, local copies, waits for them, and re-layouts: 14.5 us -> none  [the longest x2 6.72 us: gather_in_order(): parts = parts.reshape(*held, *x.shape)]
  transfers between devices with their start and end apart: 5 -> 0, of which waited for: 4 -> 0; matrix products, arithmetic and copies ran while one was open for 5% -> 0% of each run, Pallas kernels for 0% -> 0%
where the time goes in v1:
time: 70.1 us; the launch traced here: 68.8 us
  Pallas kernels  62.3 us (89%)
  local copies, waits for them, and re-layouts  5.17 us (7%)
  between operations  1.31 us (2%)
    pallas_call x1, Pallas kernels, on_device(): pl.pallas_call(functools.partial(kernel, dims), out_shape=jax.ShapeDtypeS...  62.3 us

profile of v1, /device:TPU:1, one launch (start us, length us, event | category | flops | bytes accessed | tf_op | source)
XLA Modules:
  0.0 68.8 jit_solution(11794379182231996445)
XLA Ops:
  1.3 1.3 %broadcast_in_dim.11.pos = s32[1,384]{1,0:T(1,128)} reshape(s32[384]{0:T(512)} %param.15) | data formatting | bytes 3072 | tf_op jit(solution)/shard_map/broadcast_in_dim | solution.py:338
  2.6 1.3 %broadcast_in_dim.9.bt = f32[1,1152]{1,0:T(1,128)} reshape(f32[1152]{0:T(1024)} %param.11) | data formatting | bytes 9216 | tf_op jit(solution)/shard_map/broadcast_in_dim | solution.py:338
  3.8 1.3 %broadcast_in_dim.10.bi = f32[1,1152]{1,0:T(1,128)} reshape(f32[1152]{0:T(1024)} %param.12) | data formatting | bytes 9216 | tf_op jit(solution)/shard_map/broadcast_in_dim | solution.py:338
  5.1 62.3 %shard_map.82 = f32[3,1076]{1,0:T(4,128)} custom-call(bf16[192,4304]{1,0:T(8,128)(2,1)} %bitcast.3, bf16[9,4304]{1,0:T(8,128)(2,1)} %bitcast.4, bf16[9,4304]{1,0:T(8,128)(2,1)} %bitcast.5, f32[1,1152]{1,0:T(1,128)} %broadcast_in_dim.9.bt, f32[1,1152]{1,0:T(1,128)} %broadcast_in_dim.10.bi, f32[1]{0:T(128)S(6)} %copy.10.mult, f32[1]{0:T(128)S(6)} %copy.11.off, ...), custom_call_target="tpu_custom_call" | custom-call | tf_op jit(solution)/shard_map/pallas_call | solution.py:330
  67.5 1.3 %copy.12 = f32[3,1076]{1,0:T(4,128)} copy(f32[3,1076]{1,0:T(4,128)} %shard_map.82) | data formatting | bytes 25824

commit v2 on v1

v2 whole, which is shorter than its diff:
```python
import functools

import jax
import jax.numpy as jnp
from jax import lax
from jax.experimental import pallas as pl
from jax.experimental.pallas import tpu as pltpu
from jax.sharding import Mesh
from jax.sharding import PartitionSpec as P

TXT_LEN = 64
NT = 3
K8 = 8
BF = jnp.bfloat16
F32 = jnp.float32
BLK = ("blk_0", "blk_1", "blk_2")
SECT_BLK = ("sect", "blk_0", "blk_1", "blk_2")
MESH = pl.DeviceIdType.MESH


def iota(shape, dim):
    return lax.broadcasted_iota(jnp.int32, shape, dim)


def dot_nn(a, b):
    return lax.dot_general(a, b, (((1,), (0,)), ((), ())), preferred_element_type=F32)


def dot_nt(a, b):
    return lax.dot_general(a, b, (((1,), (1,)), ((), ())), preferred_element_type=F32)


def unit_rows(p):
    inv = lax.rsqrt(jnp.sum(p * p, axis=-1, keepdims=True) + 1e-06)
    return p * inv, inv


def kernel(
    dims,
    hid, wt, wi, bt, bi, mult, off, pos,
    out,
    hv, wv, wtmp, wm, wx, xpad,
    hsend, hrecv, hall,
    pscr, psend, irecv, trecv, ifull, tfull,
    tbuf, emb, vsend, dyr, dls, osend, orecv,
    lsem, ssem, rsem, zsem,
):
    NS, NZ, NX, NY, FF = dims
    FFQ = FF // NS
    LP = wtmp.shape[1]
    NZX = NZ * NX
    NM = NZX * K8
    NE = NZX * NY
    s = lax.axis_index("sect")
    z = lax.axis_index("blk_0")
    x = lax.axis_index("blk_1")
    y = lax.axis_index("blk_2")
    zx = z * NX + x
    blk = zx * NY + y

    sect_peers = [{"sect": lax.rem(s + d, NS)} for d in range(1, NS)]
    y_far = sorted(range(1, NY), key=lambda d: -min(d, NY - d))
    y_peers = [{"blk_2": lax.rem(y + d, NY)} for d in y_far]
    z_peers = [{"blk_0": lax.rem(z + d, NZ)} for d in range(1, NZ)]
    x_peers = [{"blk_1": lax.rem(x + d, NX)} for d in range(1, NX)]
    zx_peers = []
    far = [(dz, dx) for dz in range(NZ) for dx in range(NX)][1:]
    far = sorted(far, key=lambda d: -2 * min(d[0], NZ - d[0]) - min(d[1], NX - d[1]))
    for dz, dx in far:
        zx_peers.append({"blk_0": lax.rem(z + dz, NZ), "blk_1": lax.rem(x + dx, NX)})

    loads = [
        pltpu.make_async_copy(wi, wv.at[0], lsem.at[0]),
        pltpu.make_async_copy(wt, wv.at[1], lsem.at[1]),
        pltpu.make_async_copy(hid, hv, lsem.at[2]),
    ]
    for c in loads:
        c.start()
    barrier = pltpu.get_barrier_semaphore()
    everyone = sect_peers + y_peers + x_peers + z_peers
    for p in everyone:
        pl.semaphore_signal(barrier, inc=1, device_id=p, device_id_type=MESH)

    def send(src, dst, k, peer, recv=None):
        pltpu.make_async_remote_copy(
            src_ref=src, dst_ref=dst, send_sem=ssem.at[k],
            recv_sem=rsem.at[k] if recv is None else recv,
            device_id=peer, device_id_type=MESH,
        ).start()

    def await_bytes(ref, sem):
        pltpu.make_async_copy(ref, ref, sem).wait()

    me = x * NZ + z
    for m, b in ((0, bi), (1, bt)):
        loads[m].wait()
        w32 = wv[m].astype(F32)
        wtmp[...] = jnp.zeros_like(wtmp)
        for q in range(NS):
            @pl.when(s == q)
            def _(q=q, w32=w32):
                wtmp[:, :FFQ] = w32[:, q * FFQ:(q + 1) * FFQ]
        v = wtmp[...]
        brow = jnp.broadcast_to(b[...][None], (K8 + 1, b.shape[0]))
        pick = iota(brow.shape, 1) == blk * (K8 + 1) + iota(brow.shape, 0)
        bcol = jnp.sum(jnp.where(pick, brow, 0.0), axis=1, keepdims=True)
        hi = bcol.astype(BF).astype(F32)
        lo = (bcol - hi).astype(BF).astype(F32)
        lane = iota(v.shape, 1)
        v = jnp.where(lane == FFQ, hi, v)
        v = jnp.where(lane == FFQ + 1, lo, v)
        v = jnp.where(lane == FFQ + 2, bcol - hi - lo, v)
        wm[me, m] = v[:K8].astype(BF)
        wx[me, m] = v[K8:].astype(BF).astype(F32)

    rows = hv.shape[0]
    r8 = iota((8, rows), 0)
    t8 = iota((8, rows), 1)
    is_txt = s == 0
    at = (lax.shift_right_logical(t8, 6) == r8).astype(F32)
    ai = (r8 == s - 1).astype(F32)
    f_txt = is_txt.astype(F32)
    a = (f_txt * at + (1.0 - f_txt) * ai).astype(BF)
    scale = jnp.where(is_txt, 1.0 / TXT_LEN, 1.0 / rows)
    loads[2].wait()
    hsum = dot_nn(a, hv[...]) * scale
    hsend[...] = jnp.zeros_like(hsend)
    for q in range(NS):
        hsend[q, :, :FFQ] = hsum[:4, q * FFQ:(q + 1) * FFQ].astype(BF)
    hrecv[s] = hsend[s]
    xpad[...] = jnp.zeros_like(xpad)
    dls[...] = jnp.zeros_like(dls)

    pl.semaphore_wait(barrier, len(everyone))

    for d in range(1, NS):
        send(hsend.at[lax.rem(s + d, NS)], hrecv.at[s], 0, sect_peers[d - 1])
    for i in range(NZ - 1):
        send(wm.at[me], wm.at[me], 1, z_peers[i], zsem.at[2 * i])
        send(wx.at[me], wx.at[me], 2, z_peers[i], zsem.at[2 * i + 1])
    for i in range(NX - 1):
        send(wm.at[me], wm.at[me], 3, x_peers[i])
        send(wx.at[me], wx.at[me], 4, x_peers[i])
    await_bytes(hrecv.at[pl.ds(0, NS - 1)], rsem.at[0])
    hr = hrecv[...].astype(F32)
    hq = jnp.concatenate([hr[0], hr[1] + hr[2] + hr[3]], axis=0)
    lane = iota(hq.shape, 1)
    ones = ((lane >= FFQ) & (lane < FFQ + 3)).astype(F32) * f_txt
    hall[y] = (hq + ones).astype(BF)
    for p in y_peers:
        send(hall.at[y], hall.at[y], 5, p)
    for i in range(NZ - 1):
        zz = lax.rem(z + NZ - (i + 1), NZ)
        sl = x * NZ + zz
        await_bytes(wm.at[sl], zsem.at[2 * i])
        await_bytes(wx.at[sl], zsem.at[2 * i + 1])
        for p in x_peers:
            send(wm.at[sl], wm.at[sl], 3, p)
            send(wx.at[sl], wx.at[sl], 4, p)
    await_bytes(hall.at[pl.ds(0, NY - 1)], rsem.at[5])
    hrows = hall[...].reshape(NY * 8, LP)
    nx_in = (NX - 1) * NZ
    await_bytes(wm.at[pl.ds(0, nx_in)], rsem.at[3])
    await_bytes(wx.at[pl.ds(0, nx_in)], rsem.at[4])

    parts = []
    for m in range(2):
        for j in range(NZX):
            wtmp[0:1, :] = wx[j, m]
            xpad[m, j:j + 1, :] = wtmp[0:1, :]
    for m in range(2):
        pm = dot_nt(hrows, wm[:, m].reshape(NM, LP))
        pe = dot_nt(hrows, xpad[m].astype(BF))
        parts.append((pm, pe))
    r64 = lax.bitwise_and(iota((NY * 8, 1), 0), 7)
    pe = jnp.where(r64 < 4, parts[1][1], parts[0][1])
    place = (iota((NZX, NE), 1) == y * NZX + iota((NZX, NE), 0)).astype(F32)
    pscr[:NY * 8] = jnp.where(r64 < 4, parts[1][0], parts[0][0])
    pscr[NY * 8:] = lax.dot_general(
        pe, place, (((1,), (0,)), ((), ())), preferred_element_type=F32,
        precision=lax.Precision.HIGHEST,
    )
    for r in range(NT):
        for to, row in ((r, r), (NT + r, 4 + r)):
            psend[to, :, :NM] = pscr[pl.ds(row, NY, stride=8), :]
            psend[to, :, NM:] = pscr[pl.ds(NY * 8 + row, NY, stride=8), :]

    for d in range(1, NS):
        sp = lax.rem(s + d, NS)

        @pl.when(sp != 0)
        def _(d=d, sp=sp):
            send(psend.at[NT - 1 + sp], irecv.at[s], 6, sect_peers[d - 1])

        @pl.when(sp == 0)
        def _(d=d):
            send(psend.at[pl.ds(0, NT)], trecv.at[s], 7, sect_peers[d - 1])

    m_ = mult[0]
    n_dy = NY * (NS - 1)

    @pl.when(is_txt)
    def _():
        tbuf[...] = jnp.zeros_like(tbuf)
        trecv[0] = psend[:NT]
        await_bytes(trecv.at[pl.ds(0, NS - 1)], rsem.at[7])
        tfull[y] = jnp.sum(trecv[...], axis=0)
        for p in y_peers:
            send(tfull.at[y], tfull.at[y], 8, p)
        own = iota((NY, NM + NE), 0) == y
        await_bytes(tfull.at[pl.ds(0, NY - 1)], rsem.at[8])
        for r in range(NT):
            extra = jnp.zeros((1, NE), F32)
            for j in range(NY):
                v = jnp.sum(jnp.where(own, tfull[j, r], 0.0), axis=0, keepdims=True)
                tbuf[r:r + 1, j * NM:(j + 1) * NM] = v[:, :NM]
                extra = extra + v[:, NM:]
            tbuf[r:r + 1, NY * NM:] = extra
        for i, p in enumerate(sect_peers):
            send(tbuf, tbuf, 13 + i, p, rsem.at[9])
        await_bytes(dyr, rsem.at[11])
        await_bytes(irecv.at[pl.ds(0, NS - 1)], ssem.at[6])
        await_bytes(tfull.at[pl.ds(0, NY - 1)], ssem.at[8])
        for i in range(NS - 1):
            await_bytes(tbuf, ssem.at[13 + i])

    @pl.when(jnp.logical_not(is_txt))
    def _():
        irecv[s] = psend[NT - 1 + s]
        await_bytes(irecv.at[pl.ds(0, NS - 1)], rsem.at[6])
        ifull[y] = jnp.sum(irecv[...], axis=0)
        for p in y_peers:
            send(ifull.at[y], ifull.at[y], 8, p)
        await_bytes(ifull.at[pl.ds(0, NY - 1)], rsem.at[8])
        fv = ifull[...]
        extra = jnp.sum(fv[:, :, NM:], axis=0)
        unit, _ = unit_rows(jnp.concatenate([fv[j, :, :NM] for j in range(NY)] + [extra], axis=1))
        emb[zx] = unit.astype(BF)
        for p in zx_peers:
            send(emb.at[zx], emb.at[zx], 10, p)
        NI = NZX * 8
        at_img = pos[0:NI]
        for j in range(1, NS - 1):
            at_img = jnp.where(s == j + 1, pos[j * NI:(j + 1) * NI], at_img)
        hit = at_img[None] == NT * blk + iota((4, NI), 0)
        label = jnp.where(hit, 1.0, -1.0)
        await_bytes(tbuf, rsem.at[9])
        t_unit, t_inv = unit_rows(tbuf[...])
        t_emb = t_unit.astype(BF)
        await_bytes(emb.at[pl.ds(0, NZX - 1)], rsem.at[10])
        ev = emb[...].reshape(NI, NY * NM + NE)
        logits = m_ * dot_nt(t_emb, ev) + off[0]
        coef = -label * jax.nn.sigmoid(-label * logits)
        coef = jnp.where(iota(coef.shape, 0) < NT, coef, 0.0).astype(BF)
        g = m_ * dot_nn(coef, ev)
        gp = (g - t_unit * jnp.sum(t_unit * g, axis=-1, keepdims=True)) * t_inv
        for j in range(NY):
            vsend[j, :, :NM] = gp[:, j * NM:(j + 1) * NM]
            vsend[j, :, NM:] = gp[:, NY * NM:]
        slot = y * (NS - 1) + s - 1
        dyr[slot] = vsend[y]
        for dd in y_far + [0]:
            yp = lax.rem(y + dd, NY)
            for ds in range(NS):
                if dd or ds:
                    peer = {"sect": lax.rem(s + ds, NS), "blk_2": yp}
                    send(vsend.at[yp], dyr.at[slot], 13 + ds, peer, rsem.at[11])
        await_bytes(dyr.at[pl.ds(0, n_dy - 1)], rsem.at[11])
        await_bytes(ifull.at[pl.ds(0, NY - 1)], ssem.at[8])
        await_bytes(emb.at[pl.ds(0, NZX - 1)], ssem.at[10])
        await_bytes(vsend.at[pl.ds(0, NY - 1)], ssem.at[13])
        for ds in range(1, NS):
            await_bytes(vsend, ssem.at[13 + ds])
        await_bytes(irecv.at[pl.ds(0, NS - 2)], ssem.at[6])
        await_bytes(psend.at[pl.ds(0, NT)], ssem.at[7])

    for j in range(NY):
        v = dyr[3 * j] + dyr[3 * j + 1] + dyr[3 * j + 2]
        dls[8 * j:8 * j + 4, :] = v
    dv = dls[...].astype(BF)
    take = (iota((NE, NZX), 0) == y * NZX + iota((NE, NZX), 1)).astype(F32).astype(BF)
    dext = dot_nn(dv[:, NM:], take).astype(BF)
    o = dot_nn(dv[:, :NM], wm[:, 1].reshape(NM, LP)) + dot_nn(dext, xpad[1].astype(BF))
    for j in range(NY):
        osend[j] = o[8 * j:8 * j + 4].astype(BF)
    orecv[y] = osend[y]
    for d, p in zip(y_far, y_peers):
        send(osend.at[lax.rem(y + d, NY)], orecv.at[y], 12, p)
    await_bytes(orecv.at[pl.ds(0, NY - 1)], rsem.at[12])
    out[...] = jnp.sum(orecv[...].astype(F32), axis=0)[:NT, :FFQ]

    await_bytes(hrecv.at[pl.ds(0, NS - 1)], ssem.at[0])
    await_bytes(wm.at[pl.ds(0, NZ - 1)], ssem.at[1])
    await_bytes(wx.at[pl.ds(0, NZ - 1)], ssem.at[2])
    await_bytes(wm.at[pl.ds(0, nx_in)], ssem.at[3])
    await_bytes(wx.at[pl.ds(0, nx_in)], ssem.at[4])
    await_bytes(hall.at[pl.ds(0, NY - 1)], ssem.at[5])
    await_bytes(orecv.at[pl.ds(0, NY - 1)], ssem.at[12])


def on_device(hidden, w_txt, w_img, b_txt, b_img, mult, off, pos):
    NS, NZ, NX, NY = (lax.axis_size(a) for a in SECT_BLK)
    _, rows, FF = hidden.shape
    D = b_txt.shape[0]
    K = w_txt.shape[1]
    NZX = NZ * NX
    NM, NE = NZX * K8, NZX * NY
    FFQ = FF // NS
    LP = (FFQ + 3 + 127) // 128 * 128
    dims = (NS, NZ, NX, NY, FF)
    vm = pltpu.VMEM
    scratch = [
        vm((rows, FF), BF),
        vm((2, K, FF), BF),
        vm((K, LP), F32),
        vm((NZX, 2, K8, LP), BF),
        vm((NZX, 2, 1, LP), F32),
        vm((2, NZX, LP), F32),
        vm((NS, 4, LP), BF),
        vm((NS, 4, LP), BF),
        vm((NY, 8, LP), BF),
        vm((2 * NY * 8, NM), F32),
        vm((2 * NT, NY, NM + NE), F32),
        vm((NS, NY, NM + NE), F32),
        vm((NS, NT, NY, NM + NE), F32),
        vm((NY, NY, NM + NE), F32),
        vm((NY, NT, NY, NM + NE), F32),
        vm((4, D), F32),
        vm((NZX, 8, D), BF),
        vm((NY, 4, NM + NE), F32),
        vm((NY * (NS - 1), 4, NM + NE), F32),
        vm((NY * 8, NM + NE), F32),
        vm((NY, 4, LP), BF),
        vm((NY, 4, LP), BF),
        pltpu.SemaphoreType.DMA((3,)),
        pltpu.SemaphoreType.DMA((13 + NS,)),
        pltpu.SemaphoreType.DMA((13,)),
        pltpu.SemaphoreType.DMA((2 * (NZ - 1),)),
    ]
    any_ = pl.BlockSpec(memory_space=pl.ANY)
    vmem = pl.BlockSpec(memory_space=pltpu.VMEM)
    smem = pl.BlockSpec(memory_space=pltpu.SMEM)
    return pl.pallas_call(
        functools.partial(kernel, dims),
        out_shape=jax.ShapeDtypeStruct((NT, FFQ), F32),
        in_specs=[any_, any_, any_, vmem, vmem, smem, smem, vmem],
        out_specs=vmem,
        scratch_shapes=scratch,
        compiler_params=pltpu.CompilerParams(collective_id=0, has_side_effects=True),
    )(
        hidden[0], w_txt.T, w_img.T, b_txt, b_img, mult, off, pos
    )


def solution(mesh):
    finer = Mesh(
        mesh.devices.reshape(mesh.shape["sect"], 4, 4, 8), ("sect", "blk_0", "blk_1", "blk_2")
    )
    placed = (P(SECT_BLK, None, None), P(None, BLK), P(None, BLK), P(), P(), P(), P(), P())
    return jax.shard_map(
        on_device, mesh=finer, in_specs=placed, out_specs=P(BLK, "sect"), check_vma=False
    )
```

time: 70.1 us -> 59.1 us (0.84); the launches traced: 68.8 us -> 58.8 us
  Pallas kernels: 62.3 us -> 56.2 us
  local copies, waits for them, and re-layouts: 5.17 us -> 1.33 us
    pallas_call x1, Pallas kernels: 62.3 us -> 56.2 us  [on_device(): pl.pallas_call(functools.partial(kernel, dims), out_shape=jax.ShapeDtypeS...]
    broadcast_in_dim x3 -> x0, local copies, waits for them, and re-layouts: 3.84 us -> none  [the longest x1 1.29 us: on_device(): b_txt[None]]
where the time goes in v2:
time: 59.1 us; the launch traced here: 58.8 us
  Pallas kernels  56.2 us (95%)
  local copies, waits for them, and re-layouts  1.33 us (2%)
  between operations  1.3 us (2%)
    pallas_call x1, Pallas kernels, on_device(): pl.pallas_call(functools.partial(kernel, dims), out_shape=jax.ShapeDtypeS...  56.2 us
    unnamed x1, local copies, waits for them, and re-layouts  1.33 us

profile of v2, /device:TPU:1, one launch (start us, length us, event | category | flops | bytes accessed | tf_op | source)
XLA Modules:
  0.0 58.8 jit_solution(12866763006778983854)
XLA Ops:
  1.3 56.2 %shard_map.82 = f32[3,1076]{1,0:T(4,128)} custom-call(bf16[192,4304]{1,0:T(8,128)(2,1)} %bitcast.3, bf16[9,4304]{1,0:T(8,128)(2,1)} %bitcast.4, bf16[9,4304]{1,0:T(8,128)(2,1)} %bitcast.5, f32[1152]{0:T(1024)} %bt.1, f32[1152]{0:T(1024)} %bi.1, f32[1]{0:T(128)S(6)} %copy.10.mult, f32[1]{0:T(128)S(6)} %copy.11.off, s32[384]{0:T(512)} %pos.1), custom_call_target="tpu_custom_call" | custom-call | tf_op jit(solution)/shard_map/pallas_call | solution.py:343
  57.5 1.3 %copy.12 = f32[3,1076]{1,0:T(4,128)} copy(f32[3,1076]{1,0:T(4,128)} %shard_map.82) | data formatting | bytes 25824

commit v3 on v2

--- a/solution.py
+++ b/solution.py
@@ -16,6 +16,8 @@
 BLK = ("blk_0", "blk_1", "blk_2")
 SECT_BLK = ("sect", "blk_0", "blk_1", "blk_2")
 MESH = pl.DeviceIdType.MESH
+DY = F32
+OT = F32
 
 
 def iota(shape, dim):
@@ -42,8 +44,9 @@
     hv, wv, wtmp, wm, wx, xpad,
     hsend, hrecv, hall,
     pscr, psend, irecv, trecv, ifull, tfull,
-    tbuf, emb, vsend, dyr, dls, osend, orecv,
-    lsem, ssem, rsem, zsem,
+    tbuf, emb, emit, dyr, dls, osend, orecv,
+    wf, we, wes, tm, te,
+    lsem, ssem, rsem, zsem, xsem, ysem,
 ):
     NS, NZ, NX, NY, FF = dims
     FFQ = FF // NS
@@ -62,7 +65,8 @@
     y_far = sorted(range(1, NY), key=lambda d: -min(d, NY - d))
     y_peers = [{"blk_2": lax.rem(y + d, NY)} for d in y_far]
     z_peers = [{"blk_0": lax.rem(z + d, NZ)} for d in range(1, NZ)]
-    x_peers = [{"blk_1": lax.rem(x + d, NX)} for d in range(1, NX)]
+    x_far = sorted(range(1, NX), key=lambda d: -min(d, NX - d))
+    x_peers = [{"blk_1": lax.rem(x + d, NX)} for d in x_far]
     zx_peers = []
     far = [(dz, dx) for dz in range(NZ) for dx in range(NX)][1:]
     far = sorted(far, key=lambda d: -2 * min(d[0], NZ - d[0]) - min(d[1], NX - d[1]))
@@ -110,8 +114,8 @@
         v = jnp.where(lane == FFQ, hi, v)
         v = jnp.where(lane == FFQ + 1, lo, v)
         v = jnp.where(lane == FFQ + 2, bcol - hi - lo, v)
-        wm[me, m] = v[:K8].astype(BF)
-        wx[me, m] = v[K8:].astype(BF).astype(F32)
+        wm[m, me] = v[:K8].astype(BF)
+        wx[m, me] = v[K8:].astype(BF).astype(F32)
 
     rows = hv.shape[0]
     r8 = iota((8, rows), 0)
@@ -128,6 +132,13 @@
     for q in range(NS):
         hsend[q, :, :FFQ] = hsum[:4, q * FFQ:(q + 1) * FFQ].astype(BF)
     hrecv[s] = hsend[s]
+    n_m, n_e = NY * NZ * K8, NY * NZ
+    c_m, c_e = iota((NY * NM, n_m), 1), iota((NE, n_e), 1)
+    per_y, per_z = NZ * K8, NZ
+    t_m = iota((NY * NM, n_m), 0) == c_m // per_y * NM + x * per_y + lax.rem(c_m, per_y)
+    t_e = iota((NE, n_e), 0) == c_e // per_z * NZX + x * per_z + lax.rem(c_e, per_z)
+    tm[...] = t_m.astype(F32).astype(BF)
+    te[...] = t_e.astype(F32).astype(BF)
     xpad[...] = jnp.zeros_like(xpad)
     dls[...] = jnp.zeros_like(dls)
 
@@ -135,12 +146,13 @@
 
     for d in range(1, NS):
         send(hsend.at[lax.rem(s + d, NS)], hrecv.at[s], 0, sect_peers[d - 1])
-    for i in range(NZ - 1):
-        send(wm.at[me], wm.at[me], 1, z_peers[i], zsem.at[2 * i])
-        send(wx.at[me], wx.at[me], 2, z_peers[i], zsem.at[2 * i + 1])
-    for i in range(NX - 1):
-        send(wm.at[me], wm.at[me], 3, x_peers[i])
-        send(wx.at[me], wx.at[me], 4, x_peers[i])
+    for m in range(2):
+        for i in range(NZ - 1):
+            send(wm.at[m, me], wm.at[m, me], 1, z_peers[i], zsem.at[m, i, 0])
+            send(wx.at[m, me], wx.at[m, me], 2, z_peers[i], zsem.at[m, i, 1])
+        for p in x_peers:
+            send(wm.at[m, me], wm.at[m, me], 3 + 16 * m, p, xsem.at[m, 0])
+            send(wx.at[m, me], wx.at[m, me], 4 + 16 * m, p, xsem.at[m, 1])
     await_bytes(hrecv.at[pl.ds(0, NS - 1)], rsem.at[0])
     hr = hrecv[...].astype(F32)
     hq = jnp.concatenate([hr[0], hr[1] + hr[2] + hr[3]], axis=0)
@@ -149,55 +161,74 @@
     hall[y] = (hq + ones).astype(BF)
     for p in y_peers:
         send(hall.at[y], hall.at[y], 5, p)
-    for i in range(NZ - 1):
-        zz = lax.rem(z + NZ - (i + 1), NZ)
-        sl = x * NZ + zz
-        await_bytes(wm.at[sl], zsem.at[2 * i])
-        await_bytes(wx.at[sl], zsem.at[2 * i + 1])
-        for p in x_peers:
-            send(wm.at[sl], wm.at[sl], 3, p)
-            send(wx.at[sl], wx.at[sl], 4, p)
+    for m in range(2):
+        for i in range(NZ - 1):
+            sl = x * NZ + lax.rem(z + NZ - (i + 1), NZ)
+            await_bytes(wm.at[m, sl], zsem.at[m, i, 0])
+            await_bytes(wx.at[m, sl], zsem.at[m, i, 1])
+            for p in x_peers:
+                send(wm.at[m, sl], wm.at[m, sl], 3 + 16 * m, p, xsem.at[m, 0])
+                send(wx.at[m, sl], wx.at[m, sl], 4 + 16 * m, p, xsem.at[m, 1])
     await_bytes(hall.at[pl.ds(0, NY - 1)], rsem.at[5])
     hrows = hall[...].reshape(NY * 8, LP)
     nx_in = (NX - 1) * NZ
-    await_bytes(wm.at[pl.ds(0, nx_in)], rsem.at[3])
-    await_bytes(wx.at[pl.ds(0, nx_in)], rsem.at[4])
-
-    parts = []
-    for m in range(2):
+
+    wf[y] = wm[1, pl.ds(x * NZ, NZ)].reshape(NZ * K8, LP)
+    for j in range(NZ):
+        we[y, j:j + 1, :] = wx[1, x * NZ + j]
+
+    def ring_send(t):
+        for k, far, hop in ((0, NY // 2, 1), (1, NY - 1 - NY // 2, NY - 1)):
+            if t <= far:
+                c = lax.rem(y + (NY - hop) * (t - 1), NY)
+                p = {"blk_2": lax.rem(y + hop, NY)}
+                send(wf.at[c], wf.at[c], 10 + k, p, ysem.at[k, t - 1, 0])
+                send(we.at[c], we.at[c], 14 + k, p, ysem.at[k, t - 1, 1])
+
+    def ring_wait(t):
+        for k, far, hop in ((0, NY // 2, 1), (1, NY - 1 - NY // 2, NY - 1)):
+            if t <= far:
+                c = lax.rem(y + (NY - hop) * t, NY)
+                await_bytes(wf.at[c], ysem.at[k, t - 1, 0])
+                await_bytes(we.at[c], ysem.at[k, t - 1, 1])
+
+    ring_send(1)
+
+    place = (iota((NZX, NE), 1) == y * NZX + iota((NZX, NE), 0)).astype(F32)
+
+    def tile(m, r0):
+        await_bytes(wm.at[m, pl.ds(0, nx_in)], xsem.at[m, 0])
+        await_bytes(wx.at[m, pl.ds(0, nx_in)], xsem.at[m, 1])
         for j in range(NZX):
-            wtmp[0:1, :] = wx[j, m]
-            xpad[m, j:j + 1, :] = wtmp[0:1, :]
-    for m in range(2):
-        pm = dot_nt(hrows, wm[:, m].reshape(NM, LP))
+            xpad[m, j:j + 1, :] = wx[m, j]
         pe = dot_nt(hrows, xpad[m].astype(BF))
-        parts.append((pm, pe))
-    r64 = lax.bitwise_and(iota((NY * 8, 1), 0), 7)
-    pe = jnp.where(r64 < 4, parts[1][1], parts[0][1])
-    place = (iota((NZX, NE), 1) == y * NZX + iota((NZX, NE), 0)).astype(F32)
-    pscr[:NY * 8] = jnp.where(r64 < 4, parts[1][0], parts[0][0])
-    pscr[NY * 8:] = lax.dot_general(
-        pe, place, (((1,), (0,)), ((), ())), preferred_element_type=F32,
-        precision=lax.Precision.HIGHEST,
-    )
-    for r in range(NT):
-        for to, row in ((r, r), (NT + r, 4 + r)):
-            psend[to, :, :NM] = pscr[pl.ds(row, NY, stride=8), :]
-            psend[to, :, NM:] = pscr[pl.ds(NY * 8 + row, NY, stride=8), :]
-
+        pscr[m, :NY * 8] = dot_nt(hrows, wm[m].reshape(NM, LP))
+        pscr[m, NY * 8:] = lax.dot_general(
+            pe, place, (((1,), (0,)), ((), ())), preferred_element_type=F32,
+            precision=lax.Precision.HIGHEST,
+        )
+        for r in range(NT):
+            to = r if m else NT + r
+            psend[to, :, :NM] = pscr[m, pl.ds(r0 + r, NY, stride=8), :]
+            psend[to, :, NM:] = pscr[m, pl.ds(NY * 8 + r0 + r, NY, stride=8), :]
+
+    tile(0, 4)
     for d in range(1, NS):
         sp = lax.rem(s + d, NS)
 
         @pl.when(sp != 0)
         def _(d=d, sp=sp):
             send(psend.at[NT - 1 + sp], irecv.at[s], 6, sect_peers[d - 1])
+    tile(1, 0)
+    for d in range(1, NS):
+        sp = lax.rem(s + d, NS)
 
         @pl.when(sp == 0)
         def _(d=d):
             send(psend.at[pl.ds(0, NT)], trecv.at[s], 7, sect_peers[d - 1])
 
     m_ = mult[0]
-    n_dy = NY * (NS - 1)
+    n_dy = NX * (NS - 1)
 
     @pl.when(is_txt)
     def _():
@@ -207,6 +238,8 @@
         tfull[y] = jnp.sum(trecv[...], axis=0)
         for p in y_peers:
             send(tfull.at[y], tfull.at[y], 8, p)
+        ring_wait(1)
+        ring_send(2)
         own = iota((NY, NM + NE), 0) == y
         await_bytes(tfull.at[pl.ds(0, NY - 1)], rsem.at[8])
         for r in range(NT):
@@ -217,12 +250,16 @@
                 extra = extra + v[:, NM:]
             tbuf[r:r + 1, NY * NM:] = extra
         for i, p in enumerate(sect_peers):
-            send(tbuf, tbuf, 13 + i, p, rsem.at[9])
+            send(tbuf, tbuf, 16 + i, p, rsem.at[9])
+        ring_wait(2)
+        ring_send(3)
+        ring_wait(3)
+        ring_send(4)
         await_bytes(dyr, rsem.at[11])
         await_bytes(irecv.at[pl.ds(0, NS - 1)], ssem.at[6])
         await_bytes(tfull.at[pl.ds(0, NY - 1)], ssem.at[8])
         for i in range(NS - 1):
-            await_bytes(tbuf, ssem.at[13 + i])
+            await_bytes(tbuf, ssem.at[16 + i])
 
     @pl.when(jnp.logical_not(is_txt))
     def _():
@@ -231,13 +268,17 @@
         ifull[y] = jnp.sum(irecv[...], axis=0)
         for p in y_peers:
             send(ifull.at[y], ifull.at[y], 8, p)
+        ring_wait(1)
+        ring_send(2)
         await_bytes(ifull.at[pl.ds(0, NY - 1)], rsem.at[8])
         fv = ifull[...]
         extra = jnp.sum(fv[:, :, NM:], axis=0)
         unit, _ = unit_rows(jnp.concatenate([fv[j, :, :NM] for j in range(NY)] + [extra], axis=1))
         emb[zx] = unit.astype(BF)
         for p in zx_peers:
-            send(emb.at[zx], emb.at[zx], 10, p)
+            send(emb.at[zx], emb.at[zx], 9, p, rsem.at[10])
+        ring_wait(2)
+        ring_send(3)
         NI = NZX * 8
         at_img = pos[0:NI]
         for j in range(1, NS - 1):
@@ -247,6 +288,8 @@
         await_bytes(tbuf, rsem.at[9])
         t_unit, t_inv = unit_rows(tbuf[...])
         t_emb = t_unit.astype(BF)
+        ring_wait(3)
+        ring_send(4)
         await_bytes(emb.at[pl.ds(0, NZX - 1)], rsem.at[10])
         ev = emb[...].reshape(NI, NY * NM + NE)
         logits = m_ * dot_nt(t_emb, ev) + off[0]
@@ -254,48 +297,49 @@
         coef = jnp.where(iota(coef.shape, 0) < NT, coef, 0.0).astype(BF)
         g = m_ * dot_nn(coef, ev)
         gp = (g - t_unit * jnp.sum(t_unit * g, axis=-1, keepdims=True)) * t_inv
-        for j in range(NY):
-            vsend[j, :, :NM] = gp[:, j * NM:(j + 1) * NM]
-            vsend[j, :, NM:] = gp[:, NY * NM:]
-        slot = y * (NS - 1) + s - 1
-        dyr[slot] = vsend[y]
-        for dd in y_far + [0]:
-            yp = lax.rem(y + dd, NY)
+        slot = x * (NS - 1) + s - 1
+        dyr[slot] = gp.astype(DY)
+        for dx in x_far + [0]:
             for ds in range(NS):
-                if dd or ds:
-                    peer = {"sect": lax.rem(s + ds, NS), "blk_2": yp}
-                    send(vsend.at[yp], dyr.at[slot], 13 + ds, peer, rsem.at[11])
+                if dx or ds:
+                    peer = {"sect": lax.rem(s + ds, NS), "blk_1": lax.rem(x + dx, NX)}
+                    send(dyr.at[slot], dyr.at[slot], 13, peer, rsem.at[11])
         await_bytes(dyr.at[pl.ds(0, n_dy - 1)], rsem.at[11])
         await_bytes(ifull.at[pl.ds(0, NY - 1)], ssem.at[8])
-        await_bytes(emb.at[pl.ds(0, NZX - 1)], ssem.at[10])
-        await_bytes(vsend.at[pl.ds(0, NY - 1)], ssem.at[13])
-        for ds in range(1, NS):
-            await_bytes(vsend, ssem.at[13 + ds])
+        await_bytes(emb.at[pl.ds(0, NZX - 1)], ssem.at[9])
+        await_bytes(emit.at[pl.ds(0, NX * NS - 1)], ssem.at[13])
         await_bytes(irecv.at[pl.ds(0, NS - 2)], ssem.at[6])
         await_bytes(psend.at[pl.ds(0, NT)], ssem.at[7])
 
+    for j in range(NX):
+        v = sum(dyr[(NS - 1) * j + i].astype(F32) for i in range(NS - 1))
+        dls[4 * j:4 * j + 4, :] = v
+    dv = dls[...].astype(BF)
+    d_m = dot_nn(dv[:, :NY * NM], tm[...]).astype(BF)
+    d_e = dot_nn(dv[:, NY * NM:], te[...]).astype(BF)
+    ring_wait(4)
     for j in range(NY):
-        v = dyr[3 * j] + dyr[3 * j + 1] + dyr[3 * j + 2]
-        dls[8 * j:8 * j + 4, :] = v
-    dv = dls[...].astype(BF)
-    take = (iota((NE, NZX), 0) == y * NZX + iota((NE, NZX), 1)).astype(F32).astype(BF)
-    dext = dot_nn(dv[:, NM:], take).astype(BF)
-    o = dot_nn(dv[:, :NM], wm[:, 1].reshape(NM, LP)) + dot_nn(dext, xpad[1].astype(BF))
-    for j in range(NY):
-        osend[j] = o[8 * j:8 * j + 4].astype(BF)
-    orecv[y] = osend[y]
-    for d, p in zip(y_far, y_peers):
-        send(osend.at[lax.rem(y + d, NY)], orecv.at[y], 12, p)
-    await_bytes(orecv.at[pl.ds(0, NY - 1)], rsem.at[12])
+        wes[NZ * j:NZ * (j + 1), :] = we[j]
+    o = dot_nn(d_m, wf[...].reshape(n_m, LP)) + dot_nn(d_e, wes[...].astype(BF))
+    for j in range(NX):
+        osend[j] = o[4 * j:4 * j + 4].astype(OT)
+    orecv[x] = osend[x]
+    for d, p in zip(x_far, x_peers):
+        send(osend.at[lax.rem(x + d, NX)], orecv.at[x], 12, p)
+    await_bytes(orecv.at[pl.ds(0, NX - 1)], rsem.at[12])
     out[...] = jnp.sum(orecv[...].astype(F32), axis=0)[:NT, :FFQ]
 
     await_bytes(hrecv.at[pl.ds(0, NS - 1)], ssem.at[0])
-    await_bytes(wm.at[pl.ds(0, NZ - 1)], ssem.at[1])
-    await_bytes(wx.at[pl.ds(0, NZ - 1)], ssem.at[2])
-    await_bytes(wm.at[pl.ds(0, nx_in)], ssem.at[3])
-    await_bytes(wx.at[pl.ds(0, nx_in)], ssem.at[4])
+    for k, ref in ((1, wm), (2, wx)):
+        n_z = 2 * (NZ - 1)
+        await_bytes(ref.at[0, pl.ds(0, n_z)], ssem.at[k])
+    for k, ref in ((3, wm), (4, wx), (19, wm), (20, wx)):
+        await_bytes(ref.at[0, pl.ds(0, nx_in)], ssem.at[k])
+    for k, far in ((0, NY // 2), (1, NY - 1 - NY // 2)):
+        await_bytes(wf.at[pl.ds(0, far)], ssem.at[10 + k])
+        await_bytes(we.at[pl.ds(0, far)], ssem.at[14 + k])
     await_bytes(hall.at[pl.ds(0, NY - 1)], ssem.at[5])
-    await_bytes(orecv.at[pl.ds(0, NY - 1)], ssem.at[12])
+    await_bytes(orecv.at[pl.ds(0, NX - 1)], ssem.at[12])
 
 
 def on_device(hidden, w_txt, w_img, b_txt, b_img, mult, off, pos):
@@ -313,13 +357,13 @@
         vm((rows, FF), BF),
         vm((2, K, FF), BF),
         vm((K, LP), F32),
-        vm((NZX, 2, K8, LP), BF),
-        vm((NZX, 2, 1, LP), F32),
+        vm((2, NZX, K8, LP), BF),
+        vm((2, NZX, 1, LP), F32),
         vm((2, NZX, LP), F32),
         vm((NS, 4, LP), BF),
         vm((NS, 4, LP), BF),
         vm((NY, 8, LP), BF),
-        vm((2 * NY * 8, NM), F32),
+        vm((2, 2 * NY * 8, NM), F32),
         vm((2 * NT, NY, NM + NE), F32),
         vm((NS, NY, NM + NE), F32),
         vm((NS, NT, NY, NM + NE), F32),
@@ -327,15 +371,22 @@
         vm((NY, NT, NY, NM + NE), F32),
         vm((4, D), F32),
         vm((NZX, 8, D), BF),
-        vm((NY, 4, NM + NE), F32),
-        vm((NY * (NS - 1), 4, NM + NE), F32),
-        vm((NY * 8, NM + NE), F32),
-        vm((NY, 4, LP), BF),
-        vm((NY, 4, LP), BF),
+        vm((NX * NS, 4, D), DY),
+        vm((NX * (NS - 1), 4, D), DY),
+        vm((NX * 4, D), F32),
+        vm((NX, 4, LP), OT),
+        vm((NX, 4, LP), OT),
+        vm((NY, NZ * K8, LP), BF),
+        vm((NY, NZ, LP), F32),
+        vm((NY * NZ, LP), F32),
+        vm((NY * NM, NY * NZ * K8), BF),
+        vm((NE, NY * NZ), BF),
         pltpu.SemaphoreType.DMA((3,)),
-        pltpu.SemaphoreType.DMA((13 + NS,)),
+        pltpu.SemaphoreType.DMA((21,)),
         pltpu.SemaphoreType.DMA((13,)),
-        pltpu.SemaphoreType.DMA((2 * (NZ - 1),)),
+        pltpu.SemaphoreType.DMA((2, NZ - 1, 2)),
+        pltpu.SemaphoreType.DMA((2, 2)),
+        pltpu.SemaphoreType.DMA((2, NY // 2, 2)),
     ]
     any_ = pl.BlockSpec(memory_space=pl.ANY)
     vmem = pl.BlockSpec(memory_space=pltpu.VMEM)

time: 59.1 us -> 55.3 us (0.936)
  Pallas kernels: 56.2 us -> 52.5 us
    pallas_call x1, Pallas kernels: 56.2 us -> 52.5 us  [on_device(): pl.pallas_call(functools.partial(kernel, dims), out_shape=jax.ShapeDtypeS...]
where the time goes in v3:
time: 55.3 us; the launch traced here: 55.1 us
  Pallas kernels  52.5 us (95%)
  local copies, waits for them, and re-layouts  1.33 us (2%)
  between operations  1.3 us (2%)
    pallas_call x1, Pallas kernels, on_device(): pl.pallas_call(functools.partial(kernel, dims), out_shape=jax.ShapeDtypeS...  52.5 us
    unnamed x1, local copies, waits for them, and re-layouts  1.33 us

profile of v3, /device:TPU:1, one launch (start us, length us, event | category | flops | bytes accessed | tf_op | source)
XLA Modules:
  0.0 55.1 jit_solution(13849974761159387129)
XLA Ops:
  1.3 52.5 %shard_map.82 = f32[3,1076]{1,0:T(4,128)} custom-call(bf16[192,4304]{1,0:T(8,128)(2,1)} %bitcast.3, bf16[9,4304]{1,0:T(8,128)(2,1)} %bitcast.4, bf16[9,4304]{1,0:T(8,128)(2,1)} %bitcast.5, f32[1152]{0:T(1024)} %bt.1, f32[1152]{0:T(1024)} %bi.1, f32[1]{0:T(128)S(6)} %copy.10.mult, f32[1]{0:T(128)S(6)} %copy.11.off, s32[384]{0:T(512)} %pos.1), custom_call_target="tpu_custom_call" | custom-call | tf_op jit(solution)/shard_map/pallas_call | solution.py:394
  53.8 1.3 %copy.12 = f32[3,1076]{1,0:T(4,128)} copy(f32[3,1076]{1,0:T(4,128)} %shard_map.82) | data formatting | bytes 25824

commit v4 on v3

--- a/solution.py
+++ b/solution.py
@@ -43,7 +43,7 @@
     out,
     hv, wv, wtmp, wm, wx, xpad,
     hsend, hrecv, hall,
-    pscr, psend, irecv, trecv, ifull, tfull,
+    xe, pscr, psend, ptx, irecv, trecv, ifull, tsum, tfull,
     tbuf, emb, emit, dyr, dls, osend, orecv,
     wf, we, wes, tm, te,
     lsem, ssem, rsem, zsem, xsem, ysem,
@@ -139,20 +139,25 @@
     t_e = iota((NE, n_e), 0) == c_e // per_z * NZX + x * per_z + lax.rem(c_e, per_z)
     tm[...] = t_m.astype(F32).astype(BF)
     te[...] = t_e.astype(F32).astype(BF)
-    xpad[...] = jnp.zeros_like(xpad)
+    xe[...] = jnp.zeros_like(xe)
     dls[...] = jnp.zeros_like(dls)
 
     pl.semaphore_wait(barrier, len(everyone))
 
     for d in range(1, NS):
         send(hsend.at[lax.rem(s + d, NS)], hrecv.at[s], 0, sect_peers[d - 1])
-    for m in range(2):
+    def own_z(m):
         for i in range(NZ - 1):
             send(wm.at[m, me], wm.at[m, me], 1, z_peers[i], zsem.at[m, i, 0])
             send(wx.at[m, me], wx.at[m, me], 2, z_peers[i], zsem.at[m, i, 1])
+
+    def own_x(m):
         for p in x_peers:
             send(wm.at[m, me], wm.at[m, me], 3 + 16 * m, p, xsem.at[m, 0])
-            send(wx.at[m, me], wx.at[m, me], 4 + 16 * m, p, xsem.at[m, 1])
+
+    own_z(0)
+    own_x(0)
+    own_x(1)
     await_bytes(hrecv.at[pl.ds(0, NS - 1)], rsem.at[0])
     hr = hrecv[...].astype(F32)
     hq = jnp.concatenate([hr[0], hr[1] + hr[2] + hr[3]], axis=0)
@@ -161,14 +166,19 @@
     hall[y] = (hq + ones).astype(BF)
     for p in y_peers:
         send(hall.at[y], hall.at[y], 5, p)
+    own_z(1)
     for m in range(2):
+        for i in sorted(range(NZ - 1), key=lambda i: min(i + 1, NZ - 1 - i)):
+            sl = x * NZ + lax.rem(z + NZ - (i + 1), NZ)
+            await_bytes(wm.at[m, sl], zsem.at[m, i, 0])
+            for p in x_peers:
+                send(wm.at[m, sl], wm.at[m, sl], 3 + 16 * m, p, xsem.at[m, 0])
         for i in range(NZ - 1):
             sl = x * NZ + lax.rem(z + NZ - (i + 1), NZ)
-            await_bytes(wm.at[m, sl], zsem.at[m, i, 0])
             await_bytes(wx.at[m, sl], zsem.at[m, i, 1])
-            for p in x_peers:
-                send(wm.at[m, sl], wm.at[m, sl], 3 + 16 * m, p, xsem.at[m, 0])
-                send(wx.at[m, sl], wx.at[m, sl], 4 + 16 * m, p, xsem.at[m, 1])
+        four = wx.at[m, pl.ds(x * NZ, NZ)]
+        for p in x_peers:
+            send(four, four, 4 + 16 * m, p, xsem.at[m, 1])
     await_bytes(hall.at[pl.ds(0, NY - 1)], rsem.at[5])
     hrows = hall[...].reshape(NY * 8, LP)
     nx_in = (NX - 1) * NZ
@@ -194,61 +204,57 @@
 
     ring_send(1)
 
-    place = (iota((NZX, NE), 1) == y * NZX + iota((NZX, NE), 0)).astype(F32)
-
-    def tile(m, r0):
+    def tile(m):
         await_bytes(wm.at[m, pl.ds(0, nx_in)], xsem.at[m, 0])
         await_bytes(wx.at[m, pl.ds(0, nx_in)], xsem.at[m, 1])
         for j in range(NZX):
             xpad[m, j:j + 1, :] = wx[m, j]
-        pe = dot_nt(hrows, xpad[m].astype(BF))
-        pscr[m, :NY * 8] = dot_nt(hrows, wm[m].reshape(NM, LP))
-        pscr[m, NY * 8:] = lax.dot_general(
-            pe, place, (((1,), (0,)), ((), ())), preferred_element_type=F32,
-            precision=lax.Precision.HIGHEST,
-        )
-        for r in range(NT):
-            to = r if m else NT + r
-            psend[to, :, :NM] = pscr[m, pl.ds(r0 + r, NY, stride=8), :]
-            psend[to, :, NM:] = pscr[m, pl.ds(NY * 8 + r0 + r, NY, stride=8), :]
-
-    tile(0, 4)
+        xe[m, pl.ds(pl.multiple_of(y * NZX, NZX), NZX), :] = xpad[m].astype(BF)
+        pe = dot_nt(hrows, xe[m])
+        pm = dot_nt(hrows, wm[m].reshape(NM, LP))
+        if m:
+            for j in range(NY):
+                ptx[j, :, :NM] = pm[8 * j:8 * j + 4]
+                ptx[j, :, NM:] = pe[8 * j:8 * j + 4]
+        else:
+            pscr[:NY * 8] = pm
+            pscr[NY * 8:] = pe
+            for r in range(NT):
+                psend[r, :, :NM] = pscr[pl.ds(4 + r, NY, stride=8), :]
+                psend[r, :, NM:] = pscr[pl.ds(NY * 8 + 4 + r, NY, stride=8), :]
+
+    tile(0)
     for d in range(1, NS):
         sp = lax.rem(s + d, NS)
 
         @pl.when(sp != 0)
         def _(d=d, sp=sp):
-            send(psend.at[NT - 1 + sp], irecv.at[s], 6, sect_peers[d - 1])
-    tile(1, 0)
+            send(psend.at[sp - 1], irecv.at[s], 6, sect_peers[d - 1])
+    tile(1)
     for d in range(1, NS):
         sp = lax.rem(s + d, NS)
 
         @pl.when(sp == 0)
         def _(d=d):
-            send(psend.at[pl.ds(0, NT)], trecv.at[s], 7, sect_peers[d - 1])
+            send(ptx, trecv.at[s], 7, sect_peers[d - 1])
 
     m_ = mult[0]
     n_dy = NX * (NS - 1)
 
     @pl.when(is_txt)
     def _():
-        tbuf[...] = jnp.zeros_like(tbuf)
-        trecv[0] = psend[:NT]
+        trecv[0] = ptx[...]
         await_bytes(trecv.at[pl.ds(0, NS - 1)], rsem.at[7])
-        tfull[y] = jnp.sum(trecv[...], axis=0)
-        for p in y_peers:
-            send(tfull.at[y], tfull.at[y], 8, p)
+        tsum[...] = jnp.sum(trecv[...], axis=0)
+        tfull[y] = tsum[y]
+        for d, p in zip(y_far, y_peers):
+            send(tsum.at[lax.rem(y + d, NY)], tfull.at[y], 8, p)
         ring_wait(1)
         ring_send(2)
-        own = iota((NY, NM + NE), 0) == y
         await_bytes(tfull.at[pl.ds(0, NY - 1)], rsem.at[8])
-        for r in range(NT):
-            extra = jnp.zeros((1, NE), F32)
-            for j in range(NY):
-                v = jnp.sum(jnp.where(own, tfull[j, r], 0.0), axis=0, keepdims=True)
-                tbuf[r:r + 1, j * NM:(j + 1) * NM] = v[:, :NM]
-                extra = extra + v[:, NM:]
-            tbuf[r:r + 1, NY * NM:] = extra
+        for j in range(NY):
+            tbuf[:, j * NM:(j + 1) * NM] = tfull[j, :, :NM]
+        tbuf[:, NY * NM:] = jnp.sum(tfull[:, :, NM:], axis=0)
         for i, p in enumerate(sect_peers):
             send(tbuf, tbuf, 16 + i, p, rsem.at[9])
         ring_wait(2)
@@ -263,7 +269,7 @@
 
     @pl.when(jnp.logical_not(is_txt))
     def _():
-        irecv[s] = psend[NT - 1 + s]
+        irecv[s] = psend[s - 1]
         await_bytes(irecv.at[pl.ds(0, NS - 1)], rsem.at[6])
         ifull[y] = jnp.sum(irecv[...], axis=0)
         for p in y_peers:
@@ -309,7 +315,7 @@
         await_bytes(emb.at[pl.ds(0, NZX - 1)], ssem.at[9])
         await_bytes(emit.at[pl.ds(0, NX * NS - 1)], ssem.at[13])
         await_bytes(irecv.at[pl.ds(0, NS - 2)], ssem.at[6])
-        await_bytes(psend.at[pl.ds(0, NT)], ssem.at[7])
+        await_bytes(ptx, ssem.at[7])
 
     for j in range(NX):
         v = sum(dyr[(NS - 1) * j + i].astype(F32) for i in range(NS - 1))
@@ -363,12 +369,15 @@
         vm((NS, 4, LP), BF),
         vm((NS, 4, LP), BF),
         vm((NY, 8, LP), BF),
-        vm((2, 2 * NY * 8, NM), F32),
-        vm((2 * NT, NY, NM + NE), F32),
+        vm((2, NE, LP), BF),
+        vm((2 * NY * 8, NM), F32),
+        vm((NT, NY, NM + NE), F32),
+        vm((NY, 4, NM + NE), F32),
         vm((NS, NY, NM + NE), F32),
-        vm((NS, NT, NY, NM + NE), F32),
+        vm((NS, NY, 4, NM + NE), F32),
         vm((NY, NY, NM + NE), F32),
-        vm((NY, NT, NY, NM + NE), F32),
+        vm((NY, 4, NM + NE), F32),
+        vm((NY, 4, NM + NE), F32),
         vm((4, D), F32),
         vm((NZX, 8, D), BF),
         vm((NX * NS, 4, D), DY),

time: 55.3 us -> 54.5 us (0.986)
  Pallas kernels: 52.5 us -> 51.6 us
    pallas_call x1, Pallas kernels: 52.5 us -> 51.6 us  [on_device(): pl.pallas_call(functools.partial(kernel, dims), out_shape=jax.ShapeDtypeS...]
where the time goes in v4:
time: 54.5 us; the launch traced here: 54.2 us
  Pallas kernels  51.6 us (95%)
  local copies, waits for them, and re-layouts  1.33 us (2%)
  between operations  1.3 us (2%)
    pallas_call x1, Pallas kernels, on_device(): pl.pallas_call(functools.partial(kernel, dims), out_shape=jax.ShapeDtypeS...  51.6 us
    unnamed x1, local copies, waits for them, and re-layouts  1.33 us

profile of v4, /device:TPU:1, one launch (start us, length us, event | category | flops | bytes accessed | tf_op | source)
XLA Modules:
  0.0 54.2 jit_solution(10941881559065222355)
XLA Ops:
  1.3 51.6 %shard_map.82 = f32[3,1076]{1,0:T(4,128)} custom-call(bf16[192,4304]{1,0:T(8,128)(2,1)} %bitcast.3, bf16[9,4304]{1,0:T(8,128)(2,1)} %bitcast.4, bf16[9,4304]{1,0:T(8,128)(2,1)} %bitcast.5, f32[1152]{0:T(1024)} %bt.1, f32[1152]{0:T(1024)} %bi.1, f32[1]{0:T(128)S(6)} %copy.10.mult, f32[1]{0:T(128)S(6)} %copy.11.off, s32[384]{0:T(512)} %pos.1), custom_call_target="tpu_custom_call" | custom-call | tf_op jit(solution)/shard_map/pallas_call | solution.py:403
  52.9 1.3 %copy.12 = f32[3,1076]{1,0:T(4,128)} copy(f32[3,1076]{1,0:T(4,128)} %shard_map.82) | data formatting | bytes 25824

commit v5 on v4

--- a/solution.py
+++ b/solution.py
@@ -39,14 +39,14 @@
 
 def kernel(
     dims,
-    hid, wt, wi, bt, bi, mult, off, pos,
+    hid, wt, wi, bt_hbm, bi_hbm, mult, off, pos_hbm,
     out,
     hv, wv, wtmp, wm, wx, xpad,
     hsend, hrecv, hall,
     xe, pscr, psend, ptx, irecv, trecv, ifull, tsum, tfull,
     tbuf, emb, emit, dyr, dls, osend, orecv,
     wf, we, wes, tm, te,
-    lsem, ssem, rsem, zsem, xsem, ysem,
+    bt, bi, pos, lsem, ssem, rsem, zsem, xsem, ysem,
 ):
     NS, NZ, NX, NY, FF = dims
     FFQ = FF // NS
@@ -77,6 +77,9 @@
         pltpu.make_async_copy(wi, wv.at[0], lsem.at[0]),
         pltpu.make_async_copy(wt, wv.at[1], lsem.at[1]),
         pltpu.make_async_copy(hid, hv, lsem.at[2]),
+        pltpu.make_async_copy(bi_hbm, bi, lsem.at[3]),
+        pltpu.make_async_copy(bt_hbm, bt, lsem.at[4]),
+        pltpu.make_async_copy(pos_hbm, pos, lsem.at[5]),
     ]
     for c in loads:
         c.start()
@@ -98,6 +101,7 @@
     me = x * NZ + z
     for m, b in ((0, bi), (1, bt)):
         loads[m].wait()
+        loads[3 + m].wait()
         w32 = wv[m].astype(F32)
         wtmp[...] = jnp.zeros_like(wtmp)
         for q in range(NS):
@@ -127,6 +131,7 @@
     a = (f_txt * at + (1.0 - f_txt) * ai).astype(BF)
     scale = jnp.where(is_txt, 1.0 / TXT_LEN, 1.0 / rows)
     loads[2].wait()
+    loads[5].wait()
     hsum = dot_nn(a, hv[...]) * scale
     hsend[...] = jnp.zeros_like(hsend)
     for q in range(NS):
@@ -390,7 +395,10 @@
         vm((NY * NZ, LP), F32),
         vm((NY * NM, NY * NZ * K8), BF),
         vm((NE, NY * NZ), BF),
-        pltpu.SemaphoreType.DMA((3,)),
+        vm((D,), F32),
+        vm((D,), F32),
+        vm(pos.shape, jnp.int32),
+        pltpu.SemaphoreType.DMA((6,)),
         pltpu.SemaphoreType.DMA((21,)),
         pltpu.SemaphoreType.DMA((13,)),
         pltpu.SemaphoreType.DMA((2, NZ - 1, 2)),
@@ -402,8 +410,8 @@
     smem = pl.BlockSpec(memory_space=pltpu.SMEM)
     return pl.pallas_call(
         functools.partial(kernel, dims),
-        out_shape=jax.ShapeDtypeStruct((NT, FFQ), F32),
-        in_specs=[any_, any_, any_, vmem, vmem, smem, smem, vmem],
+        out_shape=pltpu.VMEM((NT, FFQ), F32),
+        in_specs=[any_, any_, any_, any_, any_, smem, smem, any_],
         out_specs=vmem,
         scratch_shapes=scratch,
         compiler_params=pltpu.CompilerParams(collective_id=0, has_side_effects=True),

time: 54.5 us -> 52.7 us (0.967)
  Pallas kernels: 51.6 us -> 50.6 us
  local copies, waits for them, and re-layouts: 1.33 us -> 0.61 us
    pallas_call x1, Pallas kernels: 51.6 us -> 50.6 us  [on_device(): pl.pallas_call(functools.partial(kernel, dims), out_shape=pltpu.VMEM((NT,...]
    unnamed x1, local copies, waits for them, and re-layouts: 1.33 us -> 0.61 us
where the time goes in v5:
time: 52.7 us; the launch traced here: 52.5 us
  Pallas kernels  50.6 us (96%)
  between operations  1.3 us (2%)
  local copies, waits for them, and re-layouts  0.61 us (1%)
    pallas_call x1, Pallas kernels, on_device(): pl.pallas_call(functools.partial(kernel, dims), out_shape=pltpu.VMEM((NT,...  50.6 us

profile of v5, /device:TPU:1, one launch (start us, length us, event | category | flops | bytes accessed | tf_op | source)
XLA Modules:
  0.0 52.5 jit_solution(8162855347590284596)
XLA Ops:
  1.3 50.6 %shard_map.82 = f32[3,1076]{1,0:T(4,128)S(1)} custom-call(bf16[192,4304]{1,0:T(8,128)(2,1)} %bitcast.3, bf16[9,4304]{1,0:T(8,128)(2,1)} %bitcast.4, bf16[9,4304]{1,0:T(8,128)(2,1)} %bitcast.5, f32[1152]{0:T(1024)} %bt_hbm.1, f32[1152]{0:T(1024)} %bi_hbm.1, f32[1]{0:T(128)S(6)} %copy.11.mult, f32[1]{0:T(128)S(6)} %copy.12.off, s32[384]{0:T(512)} %pos_hbm.1), custom_call_target="tpu_custom_call" | custom-call | tf_op jit(solution)/shard_map/pallas_call | solution.py:411
  51.9 0.6 %copy.10 = f32[3,1076]{1,0:T(4,128)} copy(f32[3,1076]{1,0:T(4,128)S(1)} %shard_map.82) | data formatting | bytes 25824

commit v6 on v5

--- a/solution.py
+++ b/solution.py
@@ -45,7 +45,7 @@
     hsend, hrecv, hall,
     xe, pscr, psend, ptx, irecv, trecv, ifull, tsum, tfull,
     tbuf, emb, emit, dyr, dls, osend, orecv,
-    wf, we, wes, tm, te,
+    wf, we, wes,
     bt, bi, pos, lsem, ssem, rsem, zsem, xsem, ysem,
 ):
     NS, NZ, NX, NY, FF = dims
@@ -137,13 +137,6 @@
     for q in range(NS):
         hsend[q, :, :FFQ] = hsum[:4, q * FFQ:(q + 1) * FFQ].astype(BF)
     hrecv[s] = hsend[s]
-    n_m, n_e = NY * NZ * K8, NY * NZ
-    c_m, c_e = iota((NY * NM, n_m), 1), iota((NE, n_e), 1)
-    per_y, per_z = NZ * K8, NZ
-    t_m = iota((NY * NM, n_m), 0) == c_m // per_y * NM + x * per_y + lax.rem(c_m, per_y)
-    t_e = iota((NE, n_e), 0) == c_e // per_z * NZX + x * per_z + lax.rem(c_e, per_z)
-    tm[...] = t_m.astype(F32).astype(BF)
-    te[...] = t_e.astype(F32).astype(BF)
     xe[...] = jnp.zeros_like(xe)
     dls[...] = jnp.zeros_like(dls)
 
@@ -223,7 +216,7 @@
                 ptx[j, :, NM:] = pe[8 * j:8 * j + 4]
         else:
             pscr[:NY * 8] = pm
-            pscr[NY * 8:] = pe
+            pscr[NY * 8:2 * NY * 8] = pe
             for r in range(NT):
                 psend[r, :, :NM] = pscr[pl.ds(4 + r, NY, stride=8), :]
                 psend[r, :, NM:] = pscr[pl.ds(NY * 8 + 4 + r, NY, stride=8), :]
@@ -325,9 +318,23 @@
     for j in range(NX):
         v = sum(dyr[(NS - 1) * j + i].astype(F32) for i in range(NS - 1))
         dls[4 * j:4 * j + 4, :] = v
-    dv = dls[...].astype(BF)
-    d_m = dot_nn(dv[:, :NY * NM], tm[...]).astype(BF)
-    d_e = dot_nn(dv[:, NY * NM:], te[...]).astype(BF)
+    n_m, per_y = NY * NZ * K8, NZ * K8
+    lane = iota((NX * 4, NM), 1)
+    halves = []
+    for h in range(n_m // NM):
+        t = jnp.zeros((NX * 4, NM), F32)
+        for i in range(NM // per_y):
+            v = dls[:, (h * (NM // per_y) + i) * NM:(h * (NM // per_y) + i + 1) * NM]
+            v = pltpu.roll(v, lax.rem(i * per_y - x * per_y + NM, NM), 1)
+            t = jnp.where(lax.div(lane, per_y) == i, v, t)
+        halves.append(t)
+    d_m = jnp.concatenate(halves, axis=1).astype(BF)
+    v = dls[:, NY * NM:]
+    t = jnp.zeros((NX * 4, NE), F32)
+    for j in range(NY):
+        r = pltpu.roll(v, lax.rem(j * NZ - j * NZX - x * NZ + 2 * NE, NE), 1)
+        t = jnp.where(lax.div(lane, NZ) == j, r, t)
+    d_e = t[:, :NY * NZ].astype(BF)
     ring_wait(4)
     for j in range(NY):
         wes[NZ * j:NZ * (j + 1), :] = we[j]
@@ -375,7 +382,7 @@
         vm((NS, 4, LP), BF),
         vm((NY, 8, LP), BF),
         vm((2, NE, LP), BF),
-        vm((2 * NY * 8, NM), F32),
+        vm((2 * NY * 8 + 8, NM), F32),
         vm((NT, NY, NM + NE), F32),
         vm((NY, 4, NM + NE), F32),
         vm((NS, NY, NM + NE), F32),
@@ -393,8 +400,6 @@
         vm((NY, NZ * K8, LP), BF),
         vm((NY, NZ, LP), F32),
         vm((NY * NZ, LP), F32),
-        vm((NY * NM, NY * NZ * K8), BF),
-        vm((NE, NY * NZ), BF),
         vm((D,), F32),
         vm((D,), F32),
         vm(pos.shape, jnp.int32),

time: 52.7 us -> 52.3 us (level)
  no operation moved by 1% of the time
where the time goes in v6:
time: 52.3 us; the launch traced here: 52.2 us
  Pallas kernels  50.3 us (96%)
  between operations  1.3 us (2%)
  local copies, waits for them, and re-layouts  0.61 us (1%)
    pallas_call x1, Pallas kernels, on_device(): pl.pallas_call(functools.partial(kernel, dims), out_shape=pltpu.VMEM((NT,...  50.3 us

profile of v6, /device:TPU:1, one launch (start us, length us, event | category | flops | bytes accessed | tf_op | source)
XLA Modules:
  0.0 52.2 jit_solution(17328907320074398889)
XLA Ops:
  1.3 50.3 %shard_map.82 = f32[3,1076]{1,0:T(4,128)S(1)} custom-call(bf16[192,4304]{1,0:T(8,128)(2,1)} %bitcast.3, bf16[9,4304]{1,0:T(8,128)(2,1)} %bitcast.4, bf16[9,4304]{1,0:T(8,128)(2,1)} %bitcast.5, f32[1152]{0:T(1024)} %bt_hbm.1, f32[1152]{0:T(1024)} %bi_hbm.1, f32[1]{0:T(128)S(6)} %copy.11.mult, f32[1]{0:T(128)S(6)} %copy.12.off, s32[384]{0:T(512)} %pos_hbm.1), custom_call_target="tpu_custom_call" | custom-call | tf_op jit(solution)/shard_map/pallas_call | solution.py:416
  51.6 0.6 %copy.10 = f32[3,1076]{1,0:T(4,128)} copy(f32[3,1076]{1,0:T(4,128)S(1)} %shard_map.82) | data formatting | bytes 25824
